TPU v7x, 32 devices: a whole 2x2x4 slice. The times are simulated.
32 devices in a mesh: dp: 16 (over z, y, x), tensor: 2 (over core).
Axes of the slice: x: 2, y: 2, z: 4, core: 2. Of those that a mesh axis runs over, the one named last changes fastest.
Arguments:
- tokens: bfloat16 [16384, 768], P('dp'), may hold values from -6 to 6
- cotangent: bfloat16 [16384, 768], P('dp'), may hold values from -6 to 6
- w_query: bfloat16 [768, 768], P(None, 'tensor'), may hold values from -0.3125 to 0.3125
- b_query: float32 [768], P('tensor'), may hold values from -3 to 3
- w_key: bfloat16 [768, 768], P(None, 'tensor'), may hold values from -0.3125 to 0.3125
- w_value: bfloat16 [768, 768], P(None, 'tensor'), may hold values from -0.21875 to 0.21875
- b_value: float32 [768], P('tensor'), may hold values from -3 to 3
- w_out: bfloat16 [768, 768], P('tensor'), may hold values from -0.875 to 0.875
- b_out: float32 [768], replicated, may hold values from -3 to 3
- w_in: bfloat16 [768, 3072], P(None, 'tensor'), may hold values from -0.21875 to 0.21875
- b_in: float32 [3072], P('tensor'), may hold values from -3 to 3
- w_back: bfloat16 [3072, 768], P('tensor'), may hold values from -0.21875 to 0.21875
- b_back: float32 [768], replicated, may hold values from -3 to 3
- gain_attn: float32 [768], replicated, may hold values from 0.5 to 1.5
- shift_attn: float32 [768], replicated, may hold values from -2 to 2
- gain_ffn: float32 [768], replicated, may hold values from 0.5 to 1.5
- shift_ffn: float32 [768], replicated, may hold values from -2 to 2
Outputs:
- block_out: bfloat16 [16384, 768], P('dp')
- grad_tokens: float32 [16384, 768], P('dp')
- grad_w_query: float32 [768, 768], P(None, 'tensor')
- grad_b_query: float32 [768], P('tensor')
- grad_w_key: float32 [768, 768], P(None, 'tensor')
- grad_w_value: float32 [768, 768], P(None, 'tensor')
- grad_b_value: float32 [768], P('tensor')
- grad_w_out: float32 [768, 768], P('tensor')
- grad_b_out: float32 [768], replicated
- grad_w_in: float32 [768, 3072], P(None, 'tensor')
- grad_b_in: float32 [3072], P('tensor')
- grad_w_back: float32 [3072, 768], P('tensor')
- grad_b_back: float32 [768], replicated
- grad_gain_attn: float32 [768], replicated
- grad_shift_attn: float32 [768], replicated
- grad_gain_ffn: float32 [768], replicated
- grad_shift_ffn: float32 [768], replicated
All inputs are finite; a program needn't handle non-finite values.
Results may differ from a plain program's by a relative error of at most 0.015.
The roundings to bfloat16 on the way count: a program that leaves them out, or rounds other values in their place, can miss the bound.
Values may be sent and summed in bfloat16 or wider, within the bound.
A program may use at most 192 MiB of HBM per device.

v0:
```python
import jax
import jax.numpy as jnp
from jax import lax
from jax.sharding import PartitionSpec as P

HEAD = 64
SEQ = 512


EPS = 1e-12


def matmul(left, right):
    return jnp.dot(left, right, preferred_element_type=jnp.float32)


def matmul_left(left, right):
    return lax.dot_general(
        left, right, (((0,), (0,)), ((), ())), preferred_element_type=jnp.float32
    )


def matmul_right(left, right):
    return lax.dot_general(
        left, right, (((1,), (1,)), ((), ())), preferred_element_type=jnp.float32
    )


def norm_parts(value, gain, shift):
    mean = jnp.mean(value, axis=-1, keepdims=True)
    centred = value - mean
    rstd = lax.rsqrt(jnp.mean(centred * centred, axis=-1, keepdims=True) + EPS)
    unit = centred * rstd
    return (unit * gain + shift, unit, rstd)


def norm_back(grad_out, unit, rstd, gain):
    scaled = grad_out * gain
    return rstd * (
        scaled
        - jnp.mean(scaled, axis=-1, keepdims=True)
        - unit * jnp.mean(scaled * unit, axis=-1, keepdims=True)
    )


def gelu_slope(pre):
    return (
        0.5 * (1.0 + lax.erf(pre * 0.7071067811865476))
        + pre * jnp.exp(-0.5 * pre * pre) * 0.3989422804014327
    )


def flatten_all(grads):
    return jnp.concatenate([item.reshape(-1) for item in grads])


def split_back(vector, params):
    pieces = []
    offset = 0
    for item in params:
        count = item.size
        pieces.append(vector[offset : offset + count].reshape(item.shape))
        offset = offset + count
    return tuple(pieces)


def one_batch(x_rows, cot_rows, params):
    (
        w_query,
        b_query,
        w_key,
        w_value,
        b_value,
        w_out,
        b_out,
        w_in,
        b_in,
        w_back,
        b_back,
        gain_attn,
        shift_attn,
        gain_ffn,
        shift_ffn,
    ) = params
    local = w_query.shape[1]
    heads_here = local // HEAD
    scale = HEAD ** (-0.5)
    length = x_rows.shape[0]
    share = length // lax.axis_size("tensor")
    offset = lax.axis_index("tensor") * share
    xf = x_rows.astype(jnp.float32)
    x_share = lax.dynamic_slice_in_dim(xf, offset, share, 0)
    normed_f, unit_one, rstd_one = norm_parts(xf, gain_attn, shift_attn)
    normed = normed_f.astype(jnp.bfloat16)
    query = (
        (matmul(normed, w_query) + b_query).astype(jnp.bfloat16).reshape(length, heads_here, HEAD)
    )
    key = matmul(normed, w_key).astype(jnp.bfloat16).reshape(length, heads_here, HEAD)
    value = (
        (matmul(normed, w_value) + b_value).astype(jnp.bfloat16).reshape(length, heads_here, HEAD)
    )
    scores = jnp.einsum("qhd,khd->hqk", query, key, preferred_element_type=jnp.float32) * scale
    top = jnp.max(scores, axis=-1, keepdims=True)
    expo = jnp.exp(scores - top)
    total = jnp.sum(expo, axis=-1, keepdims=True)
    log_total = top + jnp.log(total)
    probs = expo / total
    mixed = (
        jnp.einsum(
            "hqk,khd->qhd", probs.astype(jnp.bfloat16), value, preferred_element_type=jnp.float32
        )
        .reshape(length, local)
        .astype(jnp.bfloat16)
    )
    attn_share = (
        lax.psum_scatter(matmul(mixed, w_out), "tensor", scatter_dimension=0, tiled=True) + b_out
    )
    hidden_share = x_share + attn_share
    normed2_f, unit_two, rstd_two = norm_parts(hidden_share, gain_ffn, shift_ffn)
    normed2 = lax.all_gather(normed2_f.astype(jnp.bfloat16), "tensor", axis=0, tiled=True)
    pre = matmul(normed2, w_in) + b_in
    act = jax.nn.gelu(pre, approximate=False).astype(jnp.bfloat16)
    ffn_share = (
        lax.psum_scatter(
            matmul(act, w_back).astype(jnp.bfloat16), "tensor", scatter_dimension=0, tiled=True
        ).astype(jnp.float32)
        + b_back
    )
    result = lax.all_gather(
        (hidden_share + ffn_share).astype(jnp.bfloat16), "tensor", axis=0, tiled=True
    )
    grad_y = cot_rows.astype(jnp.float32)
    dy_share = lax.dynamic_slice_in_dim(grad_y, offset, share, 0)
    g_b_back = jnp.sum(grad_y, axis=0)
    g_w_back = matmul_left(act, cot_rows)
    dpre = (matmul_right(cot_rows, w_back) * gelu_slope(pre)).astype(jnp.bfloat16)
    g_b_in = jnp.sum(dpre.astype(jnp.float32), axis=0)
    g_w_in = matmul_left(normed2, dpre)
    dnormed2 = lax.psum_scatter(matmul_right(dpre, w_in), "tensor", scatter_dimension=0, tiled=True)
    part_gain_ffn = jnp.sum(dnormed2 * unit_two, axis=0)
    part_shift_ffn = jnp.sum(dnormed2, axis=0)
    dhidden_share = dy_share + norm_back(dnormed2, unit_two, rstd_two, gain_ffn)
    dattn = lax.all_gather(dhidden_share.astype(jnp.bfloat16), "tensor", axis=0, tiled=True)
    g_b_out = jnp.sum(dattn.astype(jnp.float32), axis=0)
    g_w_out = matmul_left(mixed, dattn)
    dmixed = matmul_right(dattn, w_out).astype(jnp.bfloat16).reshape(length, heads_here, HEAD)
    again = jnp.einsum("qhd,khd->hqk", query, key, preferred_element_type=jnp.float32) * scale
    probs_again = jnp.exp(again - log_total)
    dprobs = jnp.einsum("qhd,khd->hqk", dmixed, value, preferred_element_type=jnp.float32)
    dscores = (
        probs_again * (dprobs - jnp.sum(dprobs * probs_again, axis=-1, keepdims=True))
    ).astype(jnp.bfloat16)
    dquery = (
        (jnp.einsum("hqk,khd->qhd", dscores, key, preferred_element_type=jnp.float32) * scale)
        .reshape(length, local)
        .astype(jnp.bfloat16)
    )
    dkey = (
        (jnp.einsum("hqk,qhd->khd", dscores, query, preferred_element_type=jnp.float32) * scale)
        .reshape(length, local)
        .astype(jnp.bfloat16)
    )
    dvalue = (
        jnp.einsum(
            "hqk,qhd->khd",
            probs_again.astype(jnp.bfloat16),
            dmixed,
            preferred_element_type=jnp.float32,
        )
        .reshape(length, local)
        .astype(jnp.bfloat16)
    )
    g_b_query = jnp.sum(dquery.astype(jnp.float32), axis=0)
    g_b_value = jnp.sum(dvalue.astype(jnp.float32), axis=0)
    g_w_query = matmul_left(normed, dquery)
    g_w_key = matmul_left(normed, dkey)
    g_w_value = matmul_left(normed, dvalue)
    dnormed = lax.psum_scatter(
        (
            matmul_right(dquery, w_query)
            + matmul_right(dkey, w_key)
            + matmul_right(dvalue, w_value)
        ).astype(jnp.bfloat16),
        "tensor",
        scatter_dimension=0,
        tiled=True,
    ).astype(jnp.float32)
    unit_one_share = lax.dynamic_slice_in_dim(unit_one, offset, share, 0)
    rstd_one_share = lax.dynamic_slice_in_dim(rstd_one, offset, share, 0)
    part_gain_attn = jnp.sum(dnormed * unit_one_share, axis=0)
    part_shift_attn = jnp.sum(dnormed, axis=0)
    grad_share = dhidden_share + norm_back(dnormed, unit_one_share, rstd_one_share, gain_attn)
    grad_x = lax.all_gather(grad_share.astype(jnp.bfloat16), "tensor", axis=0, tiled=True).astype(
        grad_share.dtype
    )
    g_gain_ffn, g_shift_ffn, g_gain_attn, g_shift_attn = lax.psum(
        (part_gain_ffn, part_shift_ffn, part_gain_attn, part_shift_attn), "tensor"
    )
    grads = (
        g_w_query,
        g_b_query,
        g_w_key,
        g_w_value,
        g_b_value,
        g_w_out,
        g_b_out,
        g_w_in,
        g_b_in,
        g_w_back,
        g_b_back,
        g_gain_attn,
        g_shift_attn,
        g_gain_ffn,
        g_shift_ffn,
    )
    return (result, grad_x, grads)


def on_device(
    tokens,
    cotangent,
    w_query,
    b_query,
    w_key,
    w_value,
    b_value,
    w_out,
    b_out,
    w_in,
    b_in,
    w_back,
    b_back,
    gain_attn,
    shift_attn,
    gain_ffn,
    shift_ffn,
):
    width = tokens.shape[1]
    params = (
        w_query,
        b_query,
        w_key,
        w_value,
        b_value,
        w_out,
        b_out,
        w_in,
        b_in,
        w_back,
        b_back,
        gain_attn,
        shift_attn,
        gain_ffn,
        shift_ffn,
    )
    inputs = tokens.reshape(-1, SEQ, width)
    cotangents = cotangent.reshape(-1, SEQ, width)
    whole_count = sum((item.size for item in params))
    start = jnp.zeros((whole_count,), jnp.float32)

    def stepper(carry, pair):
        result, grad_x, grads = one_batch(pair[0], pair[1], params)
        flat = flatten_all(grads)
        updated = carry + flat
        return (updated, (result, grad_x))

    summed, outs = lax.scan(stepper, start, (inputs, cotangents))
    summed = lax.psum_scatter(summed, "dp", scatter_dimension=0, tiled=True)
    gathered = lax.all_gather(summed.astype(jnp.bfloat16), "dp", axis=0, tiled=True).astype(
        summed.dtype
    )
    t_a, t_b, t_c, t_d, t_e, t_f, t_g, t_h, t_i, t_j, t_k, t_l, t_m, t_n, t_o = split_back(
        gathered, params
    )
    results = outs[0].reshape(-1, width)
    grad_rows = outs[1].reshape(-1, width)
    return (
        results,
        grad_rows,
        t_a,
        t_b,
        t_c,
        t_d,
        t_e,
        t_f,
        t_g,
        t_h,
        t_i,
        t_j,
        t_k,
        t_l,
        t_m,
        t_n,
        t_o,
    )


def solution(mesh):
    return jax.shard_map(
        on_device,
        mesh=mesh,
        in_specs=(
            P("dp", None),
            P("dp", None),
            P(None, "tensor"),
            P("tensor"),
            P(None, "tensor"),
            P(None, "tensor"),
            P("tensor"),
            P("tensor", None),
            P(),
            P(None, "tensor"),
            P("tensor"),
            P("tensor", None),
            P(),
            P(),
            P(),
            P(),
            P(),
        ),
        out_specs=(
            P("dp", None),
            P("dp", None),
            P(None, "tensor"),
            P("tensor"),
            P(None, "tensor"),
            P(None, "tensor"),
            P("tensor"),
            P("tensor", None),
            P(),
            P(None, "tensor"),
            P("tensor"),
            P("tensor", None),
            P(),
            P(),
            P(),
            P(),
            P(),
        ),
        check_vma=False,
    )
```

profile of v0, /device:TPU:0, one launch (start us, length us, event | category | flops | bytes accessed | tf_op | source)
XLA Modules:
  0.0 1341.8 jit_solution(4461216039275018292)
XLA Ops:
  8.1 462.9 %while.15 = (s32[]{:T(128)}, f32[3545856]{0:T(1024)}, bf16[2,512,768]{2,1,0:T(8,128)(2,1)}, f32[2,512,768]{2,1,0:T(8,128)}, bf16[2,512,768]{2,1,0:T(8,128)(2,1)}...) while((s32[]{:T(128)}, f32[3545856]{0:T(1024)}, ...), condition=%wide.region_29.30_spmd.clone, body=%wide.region_0.29_spmd.clone.sunk | while | flops 12211128320 | bytes 477097152 | solution.py:267
  22.2 10.6 reduce-scatter.5.cloned.1.call-done
  37.9 9.5 fusion.222
  72.4 5.7 reshape.324
  83.2 5.9 reshape.325
  125.9 11.3 dynamic-update-slice.53
  137.2 10.9 dynamic-update-slice.54
  149.4 10.8 dynamic-update-slice.55
  161.5 40.9 %dynamic-update-slice.56 = f32[3545856]{0:T(1024)} dynamic-update-slice(f32[3545856]{0:T(1024)} %constant_dynamic-update-slice_fusion.25, f32[1179648]{0:T(1024)} %reshape.324, s32[]{} %constant.215..sunk) | dynamic-update-slice | bytes 9437188 | tf_op jit(solution)/shard_map/while
  227.4 10.4 select_add_fusion.2
  251.9 9.0 reduce-scatter.5.cloned.1.call-done
  266.0 9.5 fusion.222
  300.5 5.7 reshape.324
  311.3 5.9 reshape.325
  354.0 11.3 dynamic-update-slice.53
  365.3 10.9 dynamic-update-slice.54
  377.5 10.8 dynamic-update-slice.55
  389.6 40.9 %dynamic-update-slice.56 = f32[3545856]{0:T(1024)} dynamic-update-slice(f32[3545856]{0:T(1024)} %constant_dynamic-update-slice_fusion.25, f32[1179648]{0:T(1024)} %reshape.324, s32[]{} %constant.215..sunk) | dynamic-update-slice | bytes 9437188 | tf_op jit(solution)/shard_map/while
  455.6 15.3 %select_add_fusion.2 = f32[3545856]{0:T(1024)} fusion(f32[3545856]{0:T(1024)} %constant_dynamic-update-slice_fusion.32, f32[3545856]{0:T(1024)} %get-tuple-element.504, pred[]{:T(512)S(6)} %compare.3), kind=kLoop, calls=%fused_computation.clone.1 | loop fusion | flops 7091712 | bytes 42550272 | tf_op jit(solution)/shard_map/while/body/eval_jaxpr/add | solution.py:264
  470.9 586.6 %all-reduce.9 = bf16[3545856]{0:T(1024)(128)(2,1)} all-reduce(f32[3545856]{0:T(1024)} %get-tuple-element.128), channel_id=6, replica_groups=mesh['dp'=16,'tensor'=2] {'dp'}, use_global_device_ids=true, to_apply=%region_30.31.clone | all-reduce | flops 3545856 | bytes 21275136
  1064.1 7.6 dynamic-update-slice
  1071.7 232.0 %all-reduce.8.cloned.1.call-done = bf16[3545856]{0:T(1024)(128)(2,1)} async-done(((bf16[3545856]{0:T(1024)(128)(2,1)}), bf16[3545856]{0:T(1024)(128)(2,1)}) %all-reduce.8.cloned.1.call-update) | async-done | bytes 7091728
  1318.6 5.8 reshape.295
  1324.4 6.0 slice.109
  (421 shorter events, 250.3 us)
Async XLA Ops:
  8.1 24.7 %reduce-scatter.5.cloned.1.call-start = ((), (), s32[]{:S(2)}) async-start(), calls=%async_computation.5 | async-start | bytes 2359296 | tf_op jit(solution)/shard_map/while/body/eval_jaxpr/reduce_scatter | solution.py:116
  11.2 49.3 %copy-start.36 = (f32[512]{0:T(512)}, f32[512]{0:T(512)S(1)}, u32[]{:S(2)}) copy-start(f32[512]{0:T(512)S(1)} %add_rsqrt_fusion.4) | copy-start | bytes 6148 | tf_op jit(solution)/shard_map/while
  19.1 13.7 %copy-start.45 = (f32[768]{0:T(1024)S(1)}, f32[768]{0:T(1024)}, u32[]{:S(2)}) copy-start(f32[768]{0:T(1024)} %get-tuple-element.547) | copy-start | bytes 9220 | tf_op jit(solution)/shard_map/while
  20.9 14.5 %copy-start.33 = (f32[768]{0:T(1024)S(1)}, f32[768]{0:T(1024)}, u32[]{:S(2)}) copy-start(f32[768]{0:T(1024)} %get-tuple-element.549) | copy-start | bytes 9220 | tf_op jit(solution)/shard_map/while
  20.9 14.4 %copy-start.46 = (f32[768]{0:T(1024)S(1)}, f32[768]{0:T(1024)}, u32[]{:S(2)}) copy-start(f32[768]{0:T(1024)} %get-tuple-element.550) | copy-start | bytes 9220 | tf_op jit(solution)/shard_map/while
  20.9 68.1 %reduce-scatter.9.cloned.1.call-start = ((), (), s32[]{:S(2)}) async-start(), calls=%async_computation.7 | async-start | bytes 1179648 | tf_op jit(solution)/shard_map/while/body/eval_jaxpr/reduce_scatter | solution.py:124
  22.2 15.7 %copy-start.54 = (f32[1536]{0:T(1024)S(1)}, f32[1536]{0:T(1024)}, u32[]{:S(2)}) copy-start(f32[1536]{0:T(1024)} %get-tuple-element.552) | copy-start | bytes 18436 | tf_op jit(solution)/shard_map/while
  50.9 38.1 %reduce-scatter.7.cloned.1.call-start = ((), (), s32[]{:S(2)}) async-start(), calls=%async_computation.6 | async-start | bytes 2359296 | tf_op jit(solution)/shard_map/while/body/eval_jaxpr/reduce_scatter | solution.py:139
  60.4 152.2 %reduce-scatter.11.cloned.1.call-start = ((), (), s32[]{:S(2)}) async-start(), calls=%async_computation.8 | async-start | bytes 1179648 | tf_op jit(solution)/shard_map/while/body/eval_jaxpr/reduce_scatter | solution.py:178
  89.0 13.2 slice-start
  161.5 40.9 %copy-start.43 = (f32[1536]{0:T(1024)S(1)}, f32[1536]{0:T(1024)}, u32[]{:S(2)}) copy-start(f32[1536]{0:T(1024)} %get-tuple-element.460) | copy-start | bytes 18436 | tf_op jit(solution)/shard_map/while
  237.8 23.1 %reduce-scatter.5.cloned.1.call-start = ((), (), s32[]{:S(2)}) async-start(), calls=%async_computation.5 | async-start | bytes 2359296 | tf_op jit(solution)/shard_map/while/body/eval_jaxpr/reduce_scatter | solution.py:116
  240.9 47.7 %copy-start.36 = (f32[512]{0:T(512)}, f32[512]{0:T(512)S(1)}, u32[]{:S(2)}) copy-start(f32[512]{0:T(512)S(1)} %add_rsqrt_fusion.4) | copy-start | bytes 6148 | tf_op jit(solution)/shard_map/while
  250.6 12.9 copy-start.33
  250.6 12.9 copy-start.46
  250.6 66.5 %reduce-scatter.9.cloned.1.call-start = ((), (), s32[]{:S(2)}) async-start(), calls=%async_computation.7 | async-start | bytes 1179648 | tf_op jit(solution)/shard_map/while/body/eval_jaxpr/reduce_scatter | solution.py:124
  251.9 14.1 %copy-start.54 = (f32[1536]{0:T(1024)S(1)}, f32[1536]{0:T(1024)}, u32[]{:S(2)}) copy-start(f32[1536]{0:T(1024)} %get-tuple-element.552) | copy-start | bytes 18436 | tf_op jit(solution)/shard_map/while
  279.0 38.1 %reduce-scatter.7.cloned.1.call-start = ((), (), s32[]{:S(2)}) async-start(), calls=%async_computation.6 | async-start | bytes 2359296 | tf_op jit(solution)/shard_map/while/body/eval_jaxpr/reduce_scatter | solution.py:139
  288.5 152.2 %reduce-scatter.11.cloned.1.call-start = ((), (), s32[]{:S(2)}) async-start(), calls=%async_computation.8 | async-start | bytes 1179648 | tf_op jit(solution)/shard_map/while/body/eval_jaxpr/reduce_scatter | solution.py:178
  317.1 13.2 slice-start
  352.6 12.8 copy-start.4
  389.6 40.9 %copy-start.43 = (f32[1536]{0:T(1024)S(1)}, f32[1536]{0:T(1024)}, u32[]{:S(2)}) copy-start(f32[1536]{0:T(1024)} %get-tuple-element.460) | copy-start | bytes 18436 | tf_op jit(solution)/shard_map/while
  470.9 832.8 %all-reduce.8.cloned.1.call-start = ((), (), s32[]{:S(2)}) async-start(), calls=%async_computation.4 | async-start | bytes 14184448
  470.9 586.6 %copy-start.48 = (u32[32]{0:T(128)S(1)}, u32[32]{0:T(128)}, u32[]{:S(2)}) copy-start(u32[32]{0:T(128)} %constant.115) | copy-start | bytes 388
  (102 other events, 458.9 us)
Sparse Core Ops, SparseCore 0:
  21.0 11.7 reduce-scatter.4
  51.0 9.4 reduce-scatter.8
  62.7 10.1 reduce-scatter.6
  116.2 9.4 reduce-scatter.10
  250.7 10.1 reduce-scatter.4
  279.1 9.4 reduce-scatter.8
  290.8 10.1 reduce-scatter.6
  344.3 9.4 reduce-scatter.10
Sparse Core Ops, SparseCore 1:
  1071.8 231.9 all-reduce.7
where the time goes:
time: 1350 us; the launch traced here: 1340 us
  blocking collectives  612 us (45%)
  local copies, waits for them, and re-layouts  276 us (20%)
  waiting for transfers between devices  252 us (19%)
  matrix products  107 us (8%)
  other arithmetic  76.4 us (6%)
  between operations  16.8 us (1%)
    unnamed x1, blocking collectives  587 us
    unnamed x2, waiting for transfers between devices  232 us
    while x260, local copies, waits for them, and re-layouts  193 us
    reshape x12, local copies, waits for them, and re-layouts, flatten_all(): return jnp.concatenate([item.reshape(-1) for item in grads])  34.9 us
    dot_general x12, matrix products, matmul(): return jnp.dot(left, right, preferred_element_type=jnp.float32)  33.9 us
    dot_general x12, matrix products, matmul_left(): lax.dot_general(left, right, (((0,), (0,)), ((), ())), preferred_element_...  27.9 us
  transfers between devices with their start and end apart: 9, of which 3 were waited for; matrix products, arithmetic and copies ran while one was open for 20% of the time, Pallas kernels for 0%

commit v1 on v0

--- a/solution.py
+++ b/solution.py
@@ -1,6 +1,10 @@
+import functools
+
 import jax
 import jax.numpy as jnp
 from jax import lax
+from jax.experimental import pallas as pl
+from jax.experimental.pallas import tpu as pltpu
 from jax.sharding import PartitionSpec as P
 
 HEAD = 64
@@ -50,18 +54,174 @@
     )
 
 
-def flatten_all(grads):
-    return jnp.concatenate([item.reshape(-1) for item in grads])
-
-
-def split_back(vector, params):
-    pieces = []
-    offset = 0
-    for item in params:
-        count = item.size
-        pieces.append(vector[offset : offset + count].reshape(item.shape))
-        offset = offset + count
-    return tuple(pieces)
+WIDE = 256
+
+
+def strides_of(bits, colour, step):
+    low = [1 << bit for bit in range(bits)]
+    if bits < 3:
+        orders = [low, low, low]
+    else:
+        orders = [low, [low[1], low[0]] + low[2:], low[2:] + low[:2]]
+    first, second, third = orders[0][step], orders[1][step], orders[2][step]
+    return jnp.where(colour == 0, first, jnp.where(colour == 1, second, third))
+
+
+def colour_of(piece):
+    return lax.rem(piece, 3)
+
+
+def reduce_kernel(bits, pieces, lag, grads, out, held, landed, load_sem, send_sem, recv_sem, free_sem, out_sem):
+    me = lax.axis_index("dp")
+    rows = held.shape[1]
+
+    def bit_at(colour, step):
+        stride = strides_of(bits, colour, step)
+        return stride, lax.rem(lax.div(me, stride), 2)
+
+    def partner_of(piece, step):
+        stride, bit = bit_at(colour_of(piece), step)
+        return me + (1 - 2 * bit) * stride
+
+    def region(colour, step):
+        base = 0
+        for earlier in range(step):
+            base = base + bit_at(colour, earlier)[1] * (rows >> (earlier + 1))
+        return base
+
+    def load(piece):
+        return pltpu.make_async_copy(grads.at[piece], held.at[piece], load_sem.at[piece])
+
+    def store(piece):
+        return pltpu.make_async_copy(held.at[piece], out.at[piece], out_sem.at[piece])
+
+    def copy(piece, step):
+        colour = colour_of(piece)
+        level = step if step < bits else 2 * bits - 1 - step
+        stride, bit = bit_at(colour, level)
+        partner = me + (1 - 2 * bit) * stride
+        half = rows >> (level + 1)
+        base = region(colour, level)
+        if step < bits:
+            start = pl.multiple_of(base + (1 - bit) * half, 16)
+            source = held.at[piece, pl.ds(start, half)]
+            target = landed.at[piece, pl.ds(rows - (rows >> level), half)]
+        else:
+            start = pl.multiple_of(base + bit * half, 16)
+            source = held.at[piece, pl.ds(start, half)]
+            target = held.at[piece, pl.ds(start, half)]
+        return pltpu.make_async_remote_copy(
+            src_ref=source,
+            dst_ref=target,
+            send_sem=send_sem.at[piece, step],
+            recv_sem=recv_sem.at[piece, step],
+            device_id={"dp": partner},
+            device_id_type=pl.DeviceIdType.MESH,
+        )
+
+    def add(piece, step):
+        colour = colour_of(piece)
+        bit = bit_at(colour, step)[1]
+        half = rows >> (step + 1)
+        start = pl.multiple_of(region(colour, step) + bit * half, 16)
+        mine = held[piece, pl.ds(start, half)].astype(jnp.float32)
+        other = landed[piece, pl.ds(rows - (rows >> step), half)].astype(jnp.float32)
+        held[piece, pl.ds(start, half)] = (mine + other).astype(held.dtype)
+
+    def advance(piece, step):
+        if step == 0:
+            load(piece).wait()
+        else:
+            copy(piece, step - 1).wait_recv()
+            if step <= bits:
+                copy(piece, step - 1).wait_send()
+                pl.semaphore_signal(
+                    free_sem.at[piece, step - 1],
+                    inc=1,
+                    device_id={"dp": partner_of(piece, step - 1)},
+                    device_id_type=pl.DeviceIdType.MESH,
+                )
+                add(piece, step - 1)
+        if step < 2 * bits:
+            if step >= bits:
+                pl.semaphore_wait(free_sem.at[piece, 2 * bits - 1 - step], 1)
+            copy(piece, step).start()
+        else:
+            store(piece).start()
+
+    barrier = pltpu.get_barrier_semaphore()
+    for bit in range(bits):
+        mine = lax.rem(lax.div(me, 1 << bit), 2)
+        pl.semaphore_signal(
+            barrier,
+            inc=1,
+            device_id={"dp": me + (1 - 2 * mine) * (1 << bit)},
+            device_id_type=pl.DeviceIdType.MESH,
+        )
+
+    def begin(piece, carry):
+        load(piece).start()
+        return carry
+
+    lax.fori_loop(0, pieces, begin, 0)
+    pl.semaphore_wait(barrier, bits)
+
+    def tick(time, carry):
+        for step in range(2 * bits + 1):
+            piece = time - lag * step
+
+            @pl.when((piece >= 0) & (piece < pieces))
+            def _():
+                advance(piece, step)
+
+        return carry
+
+    lax.fori_loop(0, pieces + lag * 2 * bits, tick, 0)
+
+    def finish(piece, carry):
+        for step in range(bits, 2 * bits):
+            copy(piece, step).wait_send()
+        store(piece).wait()
+        return carry
+
+    lax.fori_loop(0, pieces, finish, 0)
+
+
+def reduce_pieces(grads, count):
+    pieces, rows, wide = grads.shape
+    bits = count.bit_length() - 1
+    return pl.pallas_call(
+        functools.partial(reduce_kernel, bits, pieces, LAG),
+        out_shape=jax.ShapeDtypeStruct(grads.shape, grads.dtype),
+        in_specs=[pl.BlockSpec(memory_space=pl.ANY)],
+        out_specs=pl.BlockSpec(memory_space=pl.ANY),
+        scratch_shapes=[
+            pltpu.VMEM((pieces, rows, wide), grads.dtype),
+            pltpu.VMEM((pieces, rows - (rows >> bits), wide), grads.dtype),
+            pltpu.SemaphoreType.DMA((pieces,)),
+            pltpu.SemaphoreType.DMA((pieces, 2 * bits)),
+            pltpu.SemaphoreType.DMA((pieces, 2 * bits)),
+            pltpu.SemaphoreType.REGULAR((pieces, bits)),
+            pltpu.SemaphoreType.DMA((pieces,)),
+        ],
+        compiler_params=pltpu.CompilerParams(
+            collective_id=0, has_side_effects=True, vmem_limit_bytes=48 << 20
+        ),
+        name="reduce_pieces",
+    )(grads)
+
+
+LAG = 2
+
+
+def to_pieces(matrix):
+    rows, columns = matrix.shape
+    return matrix.reshape(rows, columns // WIDE, WIDE).transpose(1, 0, 2)
+
+
+def from_pieces(pieces):
+    count, rows, wide = pieces.shape
+    return pieces.transpose(1, 0, 2).reshape(rows, count * wide)
 
 
 def one_batch(x_rows, cot_rows, params):
@@ -86,6 +246,7 @@
     heads_here = local // HEAD
     scale = HEAD ** (-0.5)
     length = x_rows.shape[0]
+    seqs = length // SEQ
     share = length // lax.axis_size("tensor")
     offset = lax.axis_index("tensor") * share
     xf = x_rows.astype(jnp.float32)
@@ -93,13 +254,13 @@
     normed_f, unit_one, rstd_one = norm_parts(xf, gain_attn, shift_attn)
     normed = normed_f.astype(jnp.bfloat16)
     query = (
-        (matmul(normed, w_query) + b_query).astype(jnp.bfloat16).reshape(length, heads_here, HEAD)
-    )
-    key = matmul(normed, w_key).astype(jnp.bfloat16).reshape(length, heads_here, HEAD)
+        (matmul(normed, w_query) + b_query).astype(jnp.bfloat16).reshape(seqs, SEQ, heads_here, HEAD)
+    )
+    key = matmul(normed, w_key).astype(jnp.bfloat16).reshape(seqs, SEQ, heads_here, HEAD)
     value = (
-        (matmul(normed, w_value) + b_value).astype(jnp.bfloat16).reshape(length, heads_here, HEAD)
-    )
-    scores = jnp.einsum("qhd,khd->hqk", query, key, preferred_element_type=jnp.float32) * scale
+        (matmul(normed, w_value) + b_value).astype(jnp.bfloat16).reshape(seqs, SEQ, heads_here, HEAD)
+    )
+    scores = jnp.einsum("bqhd,bkhd->bhqk", query, key, preferred_element_type=jnp.float32) * scale
     top = jnp.max(scores, axis=-1, keepdims=True)
     expo = jnp.exp(scores - top)
     total = jnp.sum(expo, axis=-1, keepdims=True)
@@ -107,7 +268,7 @@
     probs = expo / total
     mixed = (
         jnp.einsum(
-            "hqk,khd->qhd", probs.astype(jnp.bfloat16), value, preferred_element_type=jnp.float32
+            "bhqk,bkhd->bqhd", probs.astype(jnp.bfloat16), value, preferred_element_type=jnp.float32
         )
         .reshape(length, local)
         .astype(jnp.bfloat16)
@@ -132,7 +293,7 @@
     grad_y = cot_rows.astype(jnp.float32)
     dy_share = lax.dynamic_slice_in_dim(grad_y, offset, share, 0)
     g_b_back = jnp.sum(grad_y, axis=0)
-    g_w_back = matmul_left(act, cot_rows)
+    g_w_back = matmul_left(cot_rows, act)
     dpre = (matmul_right(cot_rows, w_back) * gelu_slope(pre)).astype(jnp.bfloat16)
     g_b_in = jnp.sum(dpre.astype(jnp.float32), axis=0)
     g_w_in = matmul_left(normed2, dpre)
@@ -142,27 +303,27 @@
     dhidden_share = dy_share + norm_back(dnormed2, unit_two, rstd_two, gain_ffn)
     dattn = lax.all_gather(dhidden_share.astype(jnp.bfloat16), "tensor", axis=0, tiled=True)
     g_b_out = jnp.sum(dattn.astype(jnp.float32), axis=0)
-    g_w_out = matmul_left(mixed, dattn)
-    dmixed = matmul_right(dattn, w_out).astype(jnp.bfloat16).reshape(length, heads_here, HEAD)
-    again = jnp.einsum("qhd,khd->hqk", query, key, preferred_element_type=jnp.float32) * scale
+    g_w_out = matmul_left(dattn, mixed)
+    dmixed = matmul_right(dattn, w_out).astype(jnp.bfloat16).reshape(seqs, SEQ, heads_here, HEAD)
+    again = jnp.einsum("bqhd,bkhd->bhqk", query, key, preferred_element_type=jnp.float32) * scale
     probs_again = jnp.exp(again - log_total)
-    dprobs = jnp.einsum("qhd,khd->hqk", dmixed, value, preferred_element_type=jnp.float32)
+    dprobs = jnp.einsum("bqhd,bkhd->bhqk", dmixed, value, preferred_element_type=jnp.float32)
     dscores = (
         probs_again * (dprobs - jnp.sum(dprobs * probs_again, axis=-1, keepdims=True))
     ).astype(jnp.bfloat16)
     dquery = (
-        (jnp.einsum("hqk,khd->qhd", dscores, key, preferred_element_type=jnp.float32) * scale)
+        (jnp.einsum("bhqk,bkhd->bqhd", dscores, key, preferred_element_type=jnp.float32) * scale)
         .reshape(length, local)
         .astype(jnp.bfloat16)
     )
     dkey = (
-        (jnp.einsum("hqk,qhd->khd", dscores, query, preferred_element_type=jnp.float32) * scale)
+        (jnp.einsum("bhqk,bqhd->bkhd", dscores, query, preferred_element_type=jnp.float32) * scale)
         .reshape(length, local)
         .astype(jnp.bfloat16)
     )
     dvalue = (
         jnp.einsum(
-            "hqk,qhd->khd",
+            "bhqk,bqhd->bkhd",
             probs_again.astype(jnp.bfloat16),
             dmixed,
             preferred_element_type=jnp.float32,
@@ -253,45 +414,44 @@
         gain_ffn,
         shift_ffn,
     )
-    inputs = tokens.reshape(-1, SEQ, width)
-    cotangents = cotangent.reshape(-1, SEQ, width)
-    whole_count = sum((item.size for item in params))
-    start = jnp.zeros((whole_count,), jnp.float32)
-
-    def stepper(carry, pair):
-        result, grad_x, grads = one_batch(pair[0], pair[1], params)
-        flat = flatten_all(grads)
-        updated = carry + flat
-        return (updated, (result, grad_x))
-
-    summed, outs = lax.scan(stepper, start, (inputs, cotangents))
-    summed = lax.psum_scatter(summed, "dp", scatter_dimension=0, tiled=True)
-    gathered = lax.all_gather(summed.astype(jnp.bfloat16), "dp", axis=0, tiled=True).astype(
-        summed.dtype
-    )
-    t_a, t_b, t_c, t_d, t_e, t_f, t_g, t_h, t_i, t_j, t_k, t_l, t_m, t_n, t_o = split_back(
-        gathered, params
-    )
-    results = outs[0].reshape(-1, width)
-    grad_rows = outs[1].reshape(-1, width)
+    count = lax.axis_size("dp")
+    results, grad_rows, grads = one_batch(tokens, cotangent, params)
+    (g_wq, g_bq, g_wk, g_wv, g_bv, g_wo, g_bo, g_wi, g_bi, g_wb, g_bb, g_ga, g_sa, g_gf, g_sf) = grads
+    vectors = (g_bq, g_bv, g_bo, g_bi, g_bb, g_ga, g_sa, g_gf, g_sf)
+    sizes = [item.shape[0] for item in vectors]
+    summed = lax.psum(jnp.concatenate(vectors), "dp")
+    bounds = [sum(sizes[:i]) for i in range(len(sizes) + 1)]
+    r_bq, r_bv, r_bo, r_bi, r_bb, r_ga, r_sa, r_gf, r_sf = (
+        summed[bounds[i] : bounds[i + 1]] for i in range(len(sizes))
+    )
+    whole = jnp.concatenate([g_wi, g_wb, g_wq, g_wk, g_wv, g_wo], axis=1).astype(jnp.bfloat16)
+    if width % (16 * count) == 0 and count & (count - 1) == 0:
+        whole = from_pieces(reduce_pieces(to_pieces(whole), count))
+    else:
+        whole = lax.psum(whole, "dp")
+    whole = whole.astype(jnp.float32)
+    cuts = [0]
+    for item in (g_wi, g_wb, g_wq, g_wk, g_wv, g_wo):
+        cuts.append(cuts[-1] + item.shape[1])
+    r_wi, r_wb, r_wq, r_wk, r_wv, r_wo = (whole[:, cuts[i] : cuts[i + 1]] for i in range(6))
     return (
         results,
         grad_rows,
-        t_a,
-        t_b,
-        t_c,
-        t_d,
-        t_e,
-        t_f,
-        t_g,
-        t_h,
-        t_i,
-        t_j,
-        t_k,
-        t_l,
-        t_m,
-        t_n,
-        t_o,
+        r_wq,
+        r_bq,
+        r_wk,
+        r_wv,
+        r_bv,
+        r_wo.T,
+        r_bo,
+        r_wi,
+        r_bi,
+        r_wb.T,
+        r_bb,
+        r_ga,
+        r_sa,
+        r_gf,
+        r_sf,
     )
 
 

time: 1350 us -> 514 us (0.38)
  blocking collectives: 612 us -> 76.7 us
  waiting for transfers between devices: 252 us -> 44.6 us
  local copies, waits for them, and re-layouts: 276 us -> 91.1 us
  Pallas kernels: 0 us -> 132 us
  other arithmetic: 76.4 us -> 55 us
  matrix products: 107 us -> 93.4 us
    unnamed x1 -> x0, blocking collectives: 587 us -> none
    unnamed x2 -> x8, waiting for transfers between devices: 232 us -> 0.13 us
    while x260 -> x0, local copies, waits for them, and re-layouts: 193 us -> none
    pallas_call x0 -> x1, Pallas kernels: none -> 132 us  [reduce_pieces(): pl.pallas_call(functools.partial(reduce_kernel, bits, pieces, LAG), out_s...]
    psum x0 -> x1, blocking collectives: none -> 73.4 us  [on_device(): summed = lax.psum(jnp.concatenate(vectors), 'dp')]
    convert_element_type x0 -> x10, local copies, waits for them, and re-layouts: none -> 33.8 us  [the longest x1 15.1 us: on_device(): whole = whole.astype(jnp.float32)]
    reshape x13 -> x4, local copies, waits for them, and re-layouts: 40.7 us -> 8.27 us  [the longest x1 3.25 us: one_batch(): (matmul(normed, w_value) + b_value).astype(jnp.bfloat16)]
    add x2 -> x0, other arithmetic: 25.7 us -> none  [stepper(): updated = carry + flat]
  transfers between devices with their start and end apart: 9 -> 8, of which waited for: 3 -> 5; matrix products, arithmetic and copies ran while one was open for 20% -> 22% of each run, Pallas kernels for 0% -> 26%
where the time goes in v1:
time: 514 us; the launch traced here: 509 us
  Pallas kernels  132 us (26%)
  matrix products  93.4 us (18%)
  local copies, waits for them, and re-layouts  91.1 us (18%)
  blocking collectives  76.7 us (15%)
  other arithmetic  55 us (11%)
  waiting for transfers between devices  44.6 us (9%)
  between operations  15 us (3%)
    pallas_call x1, Pallas kernels, reduce_pieces(): pl.pallas_call(functools.partial(reduce_kernel, bits, pieces, LAG), out_s...  132 us
    psum x1, blocking collectives, on_device(): summed = lax.psum(jnp.concatenate(vectors), 'dp')  73.4 us
    dot_general x6, matrix products, matmul(): return jnp.dot(left, right, preferred_element_type=jnp.float32)  33.7 us
    unnamed x119, local copies, waits for them, and re-layouts  22.3 us
    dot_general x6, matrix products, matmul_left(): lax.dot_general(left, right, (((0,), (0,)), ((), ())), preferred_element_...  19.7 us
    dot_general x6, matrix products, matmul_right(): lax.dot_general(left, right, (((1,), (1,)), ((), ())), preferred_element_...  17.2 us
    convert_element_type x1, local copies, waits for them, and re-layouts, on_device(): whole = whole.astype(jnp.float32)  15.1 us
    transpose x2, local copies, waits for them, and re-layouts, on_device(): return (results, grad_rows, r_wq, r_bq, r_wk, r_wv, r_bv, r_wo.T, r_bo, r...  12.3 us
  transfers between devices with their start and end apart: 8, of which 5 were waited for; matrix products, arithmetic and copies ran while one was open for 22% of the time, Pallas kernels for 26%

profile of v1, /device:TPU:0, one launch (start us, length us, event | category | flops | bytes accessed | tf_op | source)
XLA Modules:
  0.0 508.9 jit_solution(11243735289695282492)
XLA Ops:
  53.4 10.5 %reduce-scatter.5.cloned.1.call-done = f32[512,768]{1,0:T(8,128)} async-done(((f32[1024,768]{1,0:T(8,128)}), f32[512,768]{1,0:T(8,128)}) %reduce-scatter.5.cloned.1.call-update) | async-done | bytes 1572880 | tf_op jit(solution)/shard_map/reduce_scatter | solution.py:277
  68.5 11.2 %all-gather.5.cloned.1.call-done = bf16[1024,768]{1,0:T(8,128)(2,1)} async-done(((bf16[512,768]{1,0:T(8,128)(2,1)}), bf16[1024,768]{1,0:T(8,128)(2,1)}) %all-gather.5.cloned.1.call-update) | async-done | bytes 1572880 | tf_op jit(solution)/shard_map/all_gather | solution.py:281
  79.6 17.5 %fusion.6 = (bf16[1024,1536]{1,0:T(8,128)(2,1)}, f32[1024,1536]{1,0:T(8,128)S(1)}) fusion(f32[1536]{0:T(1024)S(1)} %copy-done.43, bf16[1024,768]{1,0:T(8,128)(2,1)} %all-gather.5.cloned.1.call-done, bf16[768,1536]{1,0:T(8,128)(2,1)S(1)} %copy-done), kind=kOutput, calls=%fused_computation.14 | convolution fusion | flops 2519728128 | bytes 13375488 | tf_op jit(solution)/shard_map/dot_general | solution.py:18
  97.2 6.2 %convert_reduce_fusion = (f32[1536]{0:T(1024)}, bf16[1024,1536]{1,0:T(8,128)(2,1)S(1)}) fusion(f32[1024,1536]{1,0:T(8,128)S(1)} %get-tuple-element.87, f32[1536]{0:T(1024)S(1)} %copy-done.43, bf16[1024,768]{1,0:T(8,128)(2,1)S(1)} %copy-done.7, bf16[1536,768]{1,0:T(8,128)(2,1)S(1)} %copy-done.41), kind=kOutput, calls=%fused_computation.21 | convolution fusion | flops 2436364800 | bytes 13381632 | tf_op jit(solution)/shard_map/dot_general | solution.py:28
  105.1 4.3 fusion.62
  111.1 5.6 %convolution_convert_fusion.2 = bf16[1024,768]{1,0:T(8,128)(2,1)} fusion(bf16[1024,1536]{1,0:T(8,128)(2,1)} %get-tuple-element.86, bf16[1536,768]{1,0:T(8,128)(2,1)S(1)} %copy-done.42), kind=kOutput, calls=%fused_computation.58 | convolution fusion | flops 2416705536 | bytes 7077888 | tf_op jit(solution)/shard_map/dot_general | solution.py:18
  116.8 3.8 convert_element_type.147
  124.1 10.3 %reduce-scatter.7.cloned.1.call-done = bf16[512,768]{1,0:T(8,128)(2,1)} async-done(((bf16[1024,768]{1,0:T(8,128)(2,1)}), bf16[512,768]{1,0:T(8,128)(2,1)}) %reduce-scatter.7.cloned.1.call-update) | async-done | bytes 786448 | tf_op jit(solution)/shard_map/reduce_scatter | solution.py:285
  134.4 4.5 fusion.57
  139.0 11.1 %all-gather.9.cloned.1.call-done = bf16[1024,768]{1,0:T(8,128)(2,1)} async-done(((bf16[512,768]{1,0:T(8,128)(2,1)}), bf16[1024,768]{1,0:T(8,128)(2,1)}) %all-gather.9.cloned.1.call-update) | async-done | bytes 1572880 | tf_op jit(solution)/shard_map/all_gather | solution.py:304
  153.5 10.7 %multiply_reduce_fusion = (f32[2,6,512]{2,1,0:T(8,128)S(1)}, f32[2,6,512,512]{2,3,1,0:T(8,128)}) fusion(f32[2,6,512,512]{2,3,1,0:T(8,128)} %copy-done.2, f32[2,6,512]{2,1,0:T(8,128)S(1)} %log_add_fusion, bf16[2,512,6,64]{1,0,3,2:T(2,128)(2,1)S(1)} %copy-done.13, bf16[2,512,6,64]{1,0,3,2:T(2,128)(2,1)S(1)} %reshape.140), kind=kOutput, calls=%fused_computation.2 | convolution fusion | flops 415229952 | bytes 26787840 | tf_op jit(solution)/shard_map/bqhd,bkhd->bhqk/dot_general | solution.py:310
  164.2 9.9 %multiply_convert_fusion = bf16[2,6,512,512]{2,3,1,0:T(8,128)(2,1)S(1)} fusion(f32[2,6,512,512]{2,3,1,0:T(8,128)} %get-tuple-element.89, f32[2,6,512,512]{2,3,1,0:T(8,128)} %copy-done.2, f32[2,6,512]{2,1,0:T(8,128)S(1)} %get-tuple-element.88, f32[2,6,512]{2,1,0:T(8,128)S(1)} %log_add_fusion), kind=kLoop, calls=%fused_computation.1 | loop fusion | flops 15728640 | bytes 31506432 | tf_op jit(solution)/shard_map/convert_element_type | solution.py:313
  189.0 6.6 %fusion.23 = bf16[768,4608]{1,0:T(8,128)(2,1)} fusion(bf16[1024,768]{1,0:T(8,128)(2,1)} %all-gather.5.cloned.1.call-done, bf16[1024,1536]{1,0:T(8,128)(2,1)} %copy-done.46), kind=kOutput, calls=%fused_computation.43 | convolution fusion | flops 2417098752 | bytes 7077888 | tf_op jit(solution)/shard_map/dot_general | solution.py:22
  195.6 4.0 fusion.25
  199.7 3.5 fusion.42
  208.8 10.4 %copy.80 = bf16[768,4608]{0,1:T(8,128)(2,1)} copy(bf16[768,4608]{1,0:T(8,128)(2,1)} %fusion.39) | data formatting | bytes 14155776 | tf_op jit(solution)/shard_map/concatenate | solution.py:427
  219.2 10.3 %copy.81 = bf16[768,18,256]{2,0,1:T(8,128)(2,1)} copy(bf16[768,18,256]{0,2,1:T(8,128)(2,1)} %bitcast.89) | data formatting | bytes 14155776 | tf_op jit(solution)/shard_map/convert_element_type | solution.py:427
  229.5 132.3 %reduce_pieces.1 = bf16[18,768,256]{2,1,0:T(8,128)(2,1)} custom-call(bf16[18,768,256]{2,1,0:T(8,128)(2,1)} %bitcast.90), custom_call_target="tpu_custom_call" | custom-call | tf_op jit(solution)/shard_map/reduce_pieces/pallas_call | solution.py:193
  361.9 9.7 %convert_bitcast_fusion = f32[768,18,256]{2,0,1:T(8,128)} fusion(bf16[18,768,256]{2,1,0:T(8,128)(2,1)} %reduce_pieces.1), kind=kLoop, calls=%fused_computation | loop fusion | flops 3538944 | bytes 21233664 | tf_op jit(solution)/shard_map/convert_element_type | solution.py:432
  371.5 15.1 %copy.82 = f32[768,18,256]{0,2,1:T(8,128)} copy(f32[768,18,256]{2,0,1:T(8,128)} %convert_bitcast_fusion) | data formatting | bytes 28311552 | tf_op jit(solution)/shard_map/convert_element_type | solution.py:432
  386.7 8.1 %slice_bitcast_fusion = (f32[1536,768]{1,0:T(8,128)}, f32[768,1536]{0,1:T(8,128)}) fusion(f32[768,4608]{0,1:T(8,128)} %bitcast.87), kind=kLoop, calls=%fused_computation.40 | loop fusion | bytes 18874368 | tf_op jit(solution)/shard_map/transpose | solution.py:449
  394.8 4.2 slice_bitcast_fusion.1
  406.2 6.2 %copy.86 = f32[768,1536]{1,0:T(8,128)} copy(f32[768,1536]{0,1:T(8,128)} %get-tuple-element.68) | data formatting | bytes 9437184
  422.0 73.4 %psum.39 = f32[6912]{0:T(1024)S(1)} all-reduce(f32[6912]{0:T(1024)S(1)} %constant_dynamic-update-slice_fusion.4), channel_id=1, replica_groups=mesh['dp'=16,'tensor'=2] {'dp'}, use_global_device_ids=true, to_apply=%region_28.0 | all-reduce | flops 6912 | bytes 55296 | tf_op jit(solution)/shard_map/psum | solution.py:422
  (198 shorter events, 104.4 us)
Async XLA Ops:
  7.2 72.4 %copy-start = (bf16[768,1536]{1,0:T(8,128)(2,1)S(1)}, bf16[768,1536]{1,0:T(8,128)(2,1)}, u32[]{:S(2)}) copy-start(bf16[768,1536]{1,0:T(8,128)(2,1)} %param.26) | copy-start | bytes 7077892
  7.2 56.7 %reduce-scatter.5.cloned.1.call-start = ((), (), s32[]{:S(2)}) async-start(), calls=%async_computation.4 | async-start | bytes 4718592 | tf_op jit(solution)/shard_map/reduce_scatter | solution.py:277
  19.4 6.7 %copy-start.45 = (f32[384]{0:T(512)S(1)}, f32[384]{0:T(512)}, u32[]{:S(2)}) copy-start(f32[384]{0:T(512)} %param.23) | copy-start | bytes 4612
  49.9 14.1 %copy-start.40 = (f32[768]{0:T(1024)S(1)}, f32[768]{0:T(1024)}, u32[]{:S(2)}) copy-start(f32[768]{0:T(1024)} %param.25) | copy-start | bytes 9220
  49.9 29.8 %all-gather.5.cloned.1.call-start = ((), (), s32[]{:S(2)}) async-start(), calls=%async_computation.5 | async-start | bytes 2359296 | tf_op jit(solution)/shard_map/all_gather | solution.py:281
  53.4 13.8 %copy-start.29 = (f32[768]{0:T(1024)S(1)}, f32[768]{0:T(1024)}, u32[]{:S(2)}) copy-start(f32[768]{0:T(1024)} %param.32) | copy-start | bytes 9220
  53.4 13.8 %copy-start.38 = (f32[768]{0:T(1024)S(1)}, f32[768]{0:T(1024)}, u32[]{:S(2)}) copy-start(f32[768]{0:T(1024)} %param.33) | copy-start | bytes 9220
  66.1 13.6 %copy-start.43 = (f32[1536]{0:T(1024)S(1)}, f32[1536]{0:T(1024)}, u32[]{:S(2)}) copy-start(f32[1536]{0:T(1024)} %param.27) | copy-start | bytes 18436
  68.4 53.6 %reduce-scatter.9.cloned.1.call-start = ((), (), s32[]{:S(2)}) async-start(), calls=%async_computation.8 | async-start | bytes 4718592 | tf_op jit(solution)/shard_map/reduce_scatter | solution.py:300
  79.6 17.5 %copy-start.7 = (bf16[1024,768]{1,0:T(8,128)(2,1)S(1)}, bf16[1024,768]{1,0:T(8,128)(2,1)}, u32[]{:S(2)}) copy-start(bf16[1024,768]{1,0:T(8,128)(2,1)} %param.18) | copy-start | bytes 4718596
  79.6 17.5 %copy-start.41 = (bf16[1536,768]{1,0:T(8,128)(2,1)S(1)}, bf16[1536,768]{1,0:T(8,128)(2,1)}, u32[]{:S(2)}) copy-start(bf16[1536,768]{1,0:T(8,128)(2,1)} %param.28) | copy-start | bytes 7077892
  109.5 24.9 %reduce-scatter.7.cloned.1.call-start = ((), (), s32[]{:S(2)}) async-start(), calls=%async_computation.6 | async-start | bytes 2359296 | tf_op jit(solution)/shard_map/reduce_scatter | solution.py:285
  116.8 17.7 %copy-start.39 = (f32[768]{0:T(1024)S(1)}, f32[768]{0:T(1024)}, u32[]{:S(2)}) copy-start(f32[768]{0:T(1024)} %param.29) | copy-start | bytes 9220
  116.8 33.4 %all-gather.9.cloned.1.call-start = ((), (), s32[]{:S(2)}) async-start(), calls=%async_computation.9 | async-start | bytes 2359296 | tf_op jit(solution)/shard_map/all_gather | solution.py:304
  134.4 15.8 %copy-start.24 = (bf16[384,768]{1,0:T(8,128)(2,1)S(1)}, bf16[384,768]{1,0:T(8,128)(2,1)}, u32[]{:S(2)}) copy-start(bf16[384,768]{1,0:T(8,128)(2,1)} %param.24) | copy-start | bytes 1769476
  139.0 260.1 %reduce-scatter.11.cloned.1.call-start = ((), (), s32[]{:S(2)}) async-start(), calls=%async_computation.10 | async-start | bytes 2359296 | tf_op jit(solution)/shard_map/reduce_scatter | solution.py:339
  139.0 14.4 %copy-start.13 = (bf16[2,512,6,64]{1,0,3,2:T(2,128)(2,1)S(1)}, bf16[2,512,6,64]{1,0,3,2:T(2,128)(2,1)}, u32[]{:S(2)}) copy-start(bf16[2,512,6,64]{1,0,3,2:T(2,128)(2,1)} %reshape.137) | copy-start | bytes 2359300
  153.5 23.9 %slice-start = ((s8[12582912]{0:T(1024)(128)(4,1)}), s8[4194304]{0:T(1024)(128)(4,1)S(1)}, s32[]{:S(2)}) async-start(s8[12582912]{0:T(1024)(128)(4,1)} %bitcast.85), calls=%async_computation.12 | async-start | bytes 8388608
  153.5 23.8 %slice-start.1 = ((s8[12582912]{0:T(1024)(128)(4,1)}), s8[4194304]{0:T(1024)(128)(4,1)S(1)}, s32[]{:S(2)}) async-start(s8[12582912]{0:T(1024)(128)(4,1)} %bitcast.85), calls=%async_computation.13 | async-start | bytes 8388608
  164.2 13.1 %slice-start.2 = ((s8[12582912]{0:T(1024)(128)(4,1)}), s8[4194304]{0:T(1024)(128)(4,1)S(1)}, s32[]{:S(2)}) async-start(s8[12582912]{0:T(1024)(128)(4,1)} %bitcast.85), calls=%async_computation.14 | async-start | bytes 8388608
  187.8 230.3 %all-gather.7.cloned.1.call-start = ((), (), s32[]{:S(2)}) async-start(), calls=%async_computation.7 | async-start | bytes 2359296 | tf_op jit(solution)/shard_map/all_gather | solution.py:290
  199.6 297.7 %all-gather.11.cloned.1.call-start = ((), (), s32[]{:S(2)}) async-start(), calls=%async_computation.11 | async-start | bytes 2359296 | tf_op jit(solution)/shard_map/all_gather | solution.py:354
  394.8 7.2 %copy-start.34 = (f32[512]{0:T(512)S(1)}, f32[512]{0:T(512)}, u32[]{:S(2)}) copy-start(f32[512]{0:T(512)} %dynamic-slice.3) | copy-start | bytes 6148
  406.2 7.7 %copy-start.11 = (f32[768,384]{0,1:T(8,128)S(1)}, f32[768,384]{0,1:T(8,128)}, u32[]{:S(2)}) copy-start(f32[768,384]{0,1:T(8,128)} %get-tuple-element.72) | copy-start | bytes 3538948
  (35 other events, 101.9 us)
Sparse Core Ops, SparseCore 0:
  50.0 13.8 reduce-scatter.4
  68.5 11.0 all-gather.4
  109.6 12.3 reduce-scatter.8
  124.1 10.3 reduce-scatter.6
  139.1 11.0 all-gather.8
  187.9 10.2 reduce-scatter.10
  199.7 11.0 all-gather.6
  405.1 7.8 all-gather.10

commit v2 on v0

v2 whole, which is shorter than its diff:
```python
import functools

import jax
import jax.numpy as jnp
from jax import lax
from jax.experimental import pallas as pl
from jax.experimental.pallas import tpu as pltpu
from jax.sharding import PartitionSpec as P

HEAD = 64
SEQ = 512
EPS = 1e-12
SHARDS = 16
ROWS = 48
LANES = 128
LAG = 2
MESH = pl.DeviceIdType.MESH
F32 = jnp.float32
BF16 = jnp.bfloat16


def matmul(left, right):
    return jnp.dot(left, right, preferred_element_type=F32)


def matmul_left(left, right):
    return lax.dot_general(left, right, (((0,), (0,)), ((), ())), preferred_element_type=F32)


def matmul_right(left, right):
    return lax.dot_general(left, right, (((1,), (1,)), ((), ())), preferred_element_type=F32)


def norm_parts(value):
    mean = jnp.mean(value, axis=-1, keepdims=True)
    centred = value - mean
    rstd = lax.rsqrt(jnp.mean(centred * centred, axis=-1, keepdims=True) + EPS)
    return centred * rstd, rstd


def norm_back(scaled, unit, rstd):
    return rstd * (
        scaled
        - jnp.mean(scaled, axis=-1, keepdims=True)
        - unit * jnp.mean(scaled * unit, axis=-1, keepdims=True)
    )


def fold(value):
    return jnp.sum(value.reshape(value.shape[0] // 8, 8, value.shape[1]), axis=0)


class Sizes:
    def __init__(self, count, tokens, w_query, w_in):
        self.count = count
        self.bits = count.bit_length() - 1
        self.halving = min(self.bits, SHARDS.bit_length() - 1)
        self.sends = self.bits + self.halving
        self.width = tokens.shape[1]
        self.local = w_query.shape[1]
        self.hidden = w_in.shape[1]
        self.chunks = self.hidden // self.width
        self.block = self.width // LANES
        self.per_chunk = 2 * self.block
        self.first_out = self.chunks * self.per_chunk
        self.first_qkv = self.first_out + self.local // LANES
        self.pieces = self.first_qkv + 3 * self.local // LANES
        self.landing = SHARDS - (SHARDS >> self.halving) + self.bits - self.halving


def bit_orders(bits, halving):
    low = list(range(halving))
    high = list(range(halving, bits))
    if halving < 3:
        return [low + high] * 3
    return [low + high, [1, 0] + low[2:] + high, low[2:] + low[:2] + high]


def layer_kernel(
    size,
    tokens,
    cotangent,
    w_query,
    w_key,
    w_value,
    w_out,
    w_in,
    w_back,
    b_query,
    b_value,
    b_out,
    b_in,
    b_back,
    gain_attn,
    shift_attn,
    gain_ffn,
    shift_ffn,
    out_rows,
    out_grad,
    out_pieces,
    out_vectors,
    wqkv,
    wo,
    wi,
    wb,
    bias_q,
    bias_v,
    bias_i,
    x_s,
    dy_s,
    normed,
    qkv,
    mixed,
    lse,
    hidden,
    normed2,
    flip2,
    ffn,
    dn2,
    act,
    dpre,
    flip,
    wide_a,
    wide_b,
    dattn,
    dmixed,
    result,
    probs_t,
    dscores_t,
    held,
    other,
    pair,
    landed,
    vec,
    vec_other,
    vec_landed,
    load_sem,
    weight_send,
    weight_recv,
    pair_send,
    pair_recv,
    send_sem,
    recv_sem,
    free_sem,
    store_sem,
    vec_send,
    vec_recv,
    row_send,
    row_recv,
    row_sem,
):
    me = lax.axis_index("dp")
    core = lax.axis_index("tensor")
    width, local = size.width, size.local
    bits, halving, sends, pieces = size.bits, size.halving, size.sends, size.pieces
    orders = bit_orders(bits, halving)
    my_rows = pl.ds(pl.multiple_of(core * SEQ, SEQ), SEQ)

    def colour_of(piece):
        place = lax.rem(piece, 13)
        third = (place == 4) | (place == 8) | (place == 12)
        return jnp.where(third, 2, lax.rem(place, 2))

    def bit_at(colour, level):
        strides = [1 << order[level] for order in orders]
        stride = jnp.where(
            colour == 0, strides[0], jnp.where(colour == 1, strides[1], strides[2])
        )
        return stride, lax.rem(lax.div(me, stride), 2)

    def partner_of(colour, level):
        stride, bit = bit_at(colour, level)
        return me + (1 - 2 * bit) * stride

    def base_of(colour, level):
        base = 0
        for earlier in range(min(level, halving)):
            base = base + bit_at(colour, earlier)[1] * (SHARDS >> (earlier + 1))
        return base

    def landing_of(level):
        if level < halving:
            return SHARDS - (SHARDS >> level), SHARDS >> (level + 1)
        return SHARDS - (SHARDS >> halving) + level - halving, SHARDS >> halving

    def level_of(step):
        return step if step < bits else sends - 1 - step

    def copy(piece, step):
        colour = colour_of(piece)
        level = level_of(step)
        stride, bit = bit_at(colour, level)
        base = base_of(colour, level)
        if level < halving:
            half = SHARDS >> (level + 1)
            start = base + ((1 - bit) if step < bits else bit) * half
        else:
            half = SHARDS >> halving
            start = base
        source = held.at[piece, pl.ds(start, half)]
        target = source
        if step < bits:
            target = landed.at[piece, pl.ds(landing_of(level)[0], half)]
        return pltpu.make_async_remote_copy(
            src_ref=source,
            dst_ref=target,
            send_sem=send_sem.at[piece, step],
            recv_sem=recv_sem.at[piece, step],
            device_id={"dp": me + (1 - 2 * bit) * stride},
            device_id_type=MESH,
        )

    def add_level(piece, level):
        colour = colour_of(piece)
        base = base_of(colour, level + 1)
        place, half = landing_of(level)

        def one(shard, carry):
            mine = held[piece, base + shard].astype(F32)
            theirs = landed[piece, place + shard].astype(F32)
            held[piece, base + shard] = (mine + theirs).astype(BF16)
            return carry

        lax.fori_loop(0, half, one, 0)

    def pair_copy(piece):
        return pltpu.make_async_remote_copy(
            src_ref=other.at[piece],
            dst_ref=pair.at[piece],
            send_sem=pair_send.at[piece],
            recv_sem=pair_recv.at[piece],
            device_id={"tensor": 1 - core},
            device_id_type=MESH,
        )

    def store(piece):
        return pltpu.make_async_copy(held.at[piece], out_pieces.at[piece], store_sem.at[piece])

    def advance(piece, step):
        if step == 0:
            pair_copy(piece).wait_recv()

            def one(shard, carry):
                mine = held[piece, shard].astype(F32)
                held[piece, shard] = (mine + pair[piece, shard].astype(F32)).astype(BF16)
                return carry

            lax.fori_loop(0, SHARDS, one, 0)
        else:
            copy(piece, step - 1).wait_recv()
            if step <= bits:
                copy(piece, step - 1).wait_send()
                if step <= halving:
                    pl.semaphore_signal(
                        free_sem.at[piece, step - 1],
                        inc=1,
                        device_id={"dp": partner_of(colour_of(piece), step - 1)},
                        device_id_type=MESH,
                    )
                add_level(piece, step - 1)
        if step < sends:
            if step >= bits:
                pl.semaphore_wait(free_sem.at[piece, level_of(step)], 1)
            copy(piece, step).start()
        else:
            store(piece).start()

    def tick(time, carry):
        for step in range(sends + 1):
            piece = time - LAG * step

            @pl.when((piece >= 0) & (piece < pieces))
            def _():
                advance(piece, step)

        return carry

    def ticks(first, amount):
        lax.fori_loop(first, first + amount, tick, 0)

    def send_pairs(first, amount):
        def one(piece, carry):
            pair_copy(piece).start()
            return carry

        lax.fori_loop(first, first + amount, one, 0)

    def load(source, target, place):
        return pltpu.make_async_copy(source, target, load_sem.at[place])

    loads = [
        load(tokens.at[my_rows], x_s, 0),
        load(cotangent.at[my_rows], dy_s, 1),
        load(w_query, wqkv.at[0, :, pl.ds(0, local)], 2),
        load(w_key, wqkv.at[0, :, pl.ds(local, local)], 3),
        load(w_value, wqkv.at[0, :, pl.ds(2 * local, local)], 4),
        load(w_out, wo.at[pl.ds(0, local)], 5),
        load(w_in, wi.at[0], 6),
        load(w_back, wb.at[0], 7),
    ]
    for item in loads:
        item.start()

    barrier = pltpu.get_barrier_semaphore()
    pl.semaphore_signal(barrier, inc=1, device_id={"tensor": 1 - core}, device_id_type=MESH)
    for bit in range(bits):
        mine = lax.rem(lax.div(me, 1 << bit), 2)
        pl.semaphore_signal(
            barrier,
            inc=1,
            device_id={"dp": me + (1 - 2 * mine) * (1 << bit)},
            device_id_type=MESH,
        )
    pl.semaphore_wait(barrier, bits + 1)

    def to_partner(source, target, place):
        return pltpu.make_async_remote_copy(
            src_ref=source,
            dst_ref=target,
            send_sem=weight_send.at[place],
            recv_sem=weight_recv.at[place],
            device_id={"tensor": 1 - core},
            device_id_type=MESH,
        )

    gathers = [
        to_partner(b_query, bias_q, 0),
        to_partner(b_value, bias_v, 1),
        to_partner(b_in, bias_i, 2),
        to_partner(w_query, wqkv.at[1, :, pl.ds(0, local)], 3),
        to_partner(w_key, wqkv.at[1, :, pl.ds(local, local)], 4),
        to_partner(w_value, wqkv.at[1, :, pl.ds(2 * local, local)], 5),
        to_partner(w_out, wo.at[pl.ds(local, local)], 6),
        to_partner(w_in, wi.at[1], 7),
        to_partner(w_back, wb.at[1], 8),
    ]
    for item in gathers:
        item.start()

    vec[...] = jnp.zeros_like(vec)
    vec_other[...] = jnp.zeros_like(vec_other)
    ffn[...] = jnp.zeros_like(ffn)
    dn2[...] = jnp.zeros_like(dn2)

    small = 64
    loads[0].wait()

    def first_norm(tile, carry):
        rows = pl.ds(pl.multiple_of(tile * small, small), small)
        unit, rstd = norm_parts(x_s[rows].astype(F32))
        normed[rows] = (unit * gain_attn[...] + shift_attn[...]).astype(BF16)
        return carry

    lax.fori_loop(0, SEQ // small, first_norm, 0)

    for half in range(2):
        if half == 0:
            for item in loads[2:5]:
                item.wait()
            bias_query, bias_value = b_query, b_value
        else:
            for item in gathers[0:2] + gathers[3:6]:
                item.wait_recv()
            bias_query, bias_value = bias_q, bias_v
        qkv[half, :, 0:local] = (
            matmul(normed[...], wqkv[half, :, 0:local]) + bias_query[...]
        ).astype(BF16)
        qkv[half, :, local : 2 * local] = matmul(
            normed[...], wqkv[half, :, local : 2 * local]
        ).astype(BF16)
        qkv[half, :, 2 * local : 3 * local] = (
            matmul(normed[...], wqkv[half, :, 2 * local : 3 * local]) + bias_value[...]
        ).astype(BF16)

    pairs_half = local // LANES
    scale = HEAD ** (-0.5)
    lane = lax.broadcasted_iota(jnp.int32, (1, LANES), 1)
    masks = [
        jnp.where((lane >= part * HEAD) & (lane < (part + 1) * HEAD), 1.0, 0.0).astype(BF16)
        for part in range(LANES // HEAD)
    ]
    queries = 128

    def columns(index, group):
        return pl.ds(pl.multiple_of(group * local + index * LANES, LANES), LANES)

    def attend(index, carry):
        half, place = lax.div(index, pairs_half), lax.rem(index, pairs_half)
        key = qkv[half, :, columns(place, 1)]
        value = qkv[half, :, columns(place, 2)]
        total = None
        for part, mask in enumerate(masks):
            for tile in range(SEQ // queries):
                rows = slice(tile * queries, (tile + 1) * queries)
                query = qkv[half, rows, columns(place, 0)] * (mask * scale).astype(BF16)
                scores = matmul_right(key, query)
                top = jnp.max(scores, axis=0, keepdims=True)
                expo = jnp.exp(scores - top)
                amount = jnp.sum(expo, axis=0, keepdims=True)
                lse[index * 2 + part, :, rows] = top + jnp.log(amount)
                probs_t[part, :, rows] = (expo * (1.0 / amount)).astype(BF16)
            term = matmul_left(probs_t[part], value * mask)
            total = term if total is None else total + term
        mixed[:, pl.ds(pl.multiple_of(index * LANES, LANES), LANES)] = total.astype(BF16)
        return carry

    lax.fori_loop(0, 2 * pairs_half, attend, 0)

    loads[5].wait()
    gathers[6].wait_recv()
    hidden[...] = matmul(mixed[...], wo[...])

    def second_norm(tile, carry):
        rows = pl.ds(pl.multiple_of(tile * small, small), small)
        whole = x_s[rows].astype(F32) + (hidden[rows] + b_out[...])
        hidden[rows] = whole
        unit, rstd = norm_parts(whole)
        normed2[rows] = (unit * gain_ffn[...] + shift_ffn[...]).astype(BF16)
        return carry

    lax.fori_loop(0, SEQ // small, second_norm, 0)
    flip2[...] = normed2[...].T

    loads[1].wait()
    loads[6].wait()
    loads[7].wait()
    gathers[2].wait_recv()
    gathers[7].wait_recv()
    gathers[8].wait_recv()
    ones = jnp.ones((16, SEQ), BF16)
    fine = 32
    tall = 256

    def hand_in(target, first, grad, kind, part):
        wide = 2 * LANES
        if kind == "in":
            for side in range(2):
                target[first + 2 * part + side] = (
                    grad[:, side * LANES : (side + 1) * LANES]
                    .astype(BF16)
                    .reshape(SHARDS, ROWS, LANES)
                )
        else:
            blocks = grad.shape[0] // (ROWS * SHARDS // 2)
            for block in range(blocks):
                rows = slice(block * ROWS * SHARDS // 2, (block + 1) * ROWS * SHARDS // 2)
                for side in range(2):
                    target[
                        first + (width // wide) * block + part,
                        side * (SHARDS // 2) : (side + 1) * (SHARDS // 2),
                    ] = (
                        grad[rows, side * LANES : (side + 1) * LANES]
                        .astype(BF16)
                        .reshape(SHARDS // 2, ROWS, LANES)
                    )

    def feed(chunk, half, slots):
        begin = pl.multiple_of(chunk * width, width)
        units = pl.ds(begin, width)
        bias_row = b_in if half == 0 else bias_i
        target = held if half == 0 else other
        first = chunk * size.per_chunk

        def rows_tile(tile, carry):
            rows = pl.ds(pl.multiple_of(tile * tall, tall), tall)
            wide_a[...] = matmul(normed2[rows], wi[half, :, units])
            wide_b[...] = matmul_right(dy_s[rows], wb[half, units, :])

            def inner(step, carry):
                piece = pl.ds(pl.multiple_of(step * fine, fine), fine)
                there = pl.ds(pl.multiple_of(tile * tall + step * fine, fine), fine)
                pre = wide_a[piece] + bias_row[:, units]
                phi = 0.5 * (1.0 + lax.erf(pre * 0.7071067811865476))
                act[there] = (pre * phi).astype(BF16)
                slope = phi + pre * jnp.exp(-0.5 * pre * pre) * 0.3989422804014327
                dpre[there] = (wide_b[piece] * slope).astype(BF16)
                return carry

            lax.fori_loop(0, tall // fine, inner, 0)
            return carry

        lax.fori_loop(0, SEQ // tall, rows_tile, 0)
        slots(0)
        flip[...] = act[...].T
        ffn[...] += matmul(act[...], wb[half, units, :])
        slots(1)
        dn2[...] += matmul_right(dpre[...], wi[half, :, units])
        slots(2)
        for part in range(width // 256):
            cols = slice(part * 256, (part + 1) * 256)
            hand_in(target, first, matmul(flip2[...], dpre[:, cols]), "in", part)
        slots(3)
        for part in range(width // 256):
            cols = slice(part * 256, (part + 1) * 256)
            hand_in(target, first + size.block, matmul(flip[...], dy_s[:, cols]), "out", part)
        slots(4)
        sums = matmul(ones, dpre[...])[0:1]
        (vec if half == 0 else vec_other)[pl.ds(7 + chunk, 1)] = sums

    def feed_both(chunk, carry):
        def slots(offset):
            def place(index):
                first = (chunk - 1) * 10 + offset + index
                lax.fori_loop(first, jnp.where(chunk > 0, first + 1, first), tick, 0)

            return place

        feed(chunk, 1, slots(0))
        send_pairs(chunk * size.per_chunk, size.per_chunk)
        feed(chunk, 0, slots(5))
        return carry

    lax.fori_loop(0, size.chunks, feed_both, 0)
    time = 10 * (size.chunks - 1)

    tiny = 32

    def second_back(tile, carry):
        sum_gain, sum_shift, sum_out = carry
        rows = pl.ds(pl.multiple_of(tile * tiny, tiny), tiny)
        whole = hidden[rows]
        result[rows] = (whole + (ffn[rows] + b_back[...])).astype(BF16)
        unit, rstd = norm_parts(whole)
        grad = dn2[rows]
        dhidden = dy_s[rows].astype(F32) + norm_back(grad * gain_ffn[...], unit, rstd)
        dn2[rows] = dhidden
        rounded = dhidden.astype(BF16)
        dattn[rows] = rounded
        return (
            sum_gain + fold(grad * unit),
            sum_shift + fold(grad),
            sum_out + fold(rounded.astype(F32)),
        )

    zero = jnp.zeros((8, width), F32)
    sum_gain, sum_shift, sum_out = lax.fori_loop(
        0, SEQ // tiny, second_back, (zero, zero, zero)
    )

    def both(row, value):
        vec[row : row + 1] = value
        vec_other[row : row + 1] = value

    both(0, jnp.sum(sum_out, axis=0, keepdims=True))
    both(1, matmul(ones, dy_s[...])[0:1])
    both(4, jnp.sum(sum_gain, axis=0, keepdims=True))
    both(5, jnp.sum(sum_shift, axis=0, keepdims=True))

    def row_copies(source, target, place):
        return (
            pltpu.make_async_copy(source, target.at[my_rows], row_sem.at[place]),
            pltpu.make_async_remote_copy(
                src_ref=source,
                dst_ref=target.at[my_rows],
                send_sem=row_send.at[place],
                recv_sem=row_recv.at[place],
                device_id={"tensor": 1 - core},
                device_id_type=MESH,
            ),
        )

    result_copies = row_copies(result, out_rows, 0)
    for item in result_copies:
        item.start()
    ticks(time, 2)
    time += 2

    flip[...] = mixed[...].T
    for part in range(width // 256):
        cols = slice(part * 256, (part + 1) * 256)
        grad = matmul(flip[...], dattn[:, cols])
        hand_in(held, size.first_out, grad[0:local], "out", part)
        hand_in(other, size.first_out, grad[local:], "out", part)
    send_pairs(size.first_out, size.first_qkv - size.first_out)
    dmixed[...] = matmul_right(dattn[...], wo[...]).astype(BF16)
    ticks(time, 1)
    time += 1

    def attend_back(index, carry):
        half, place = lax.div(index, pairs_half), lax.rem(index, pairs_half)
        here = pl.ds(pl.multiple_of(index * LANES, LANES), LANES)
        key = qkv[half, :, columns(place, 1)]
        value = qkv[half, :, columns(place, 2)]
        dquery, dkey, dvalue = None, None, None
        for part, mask in enumerate(masks):
            for tile in range(SEQ // queries):
                rows = slice(tile * queries, (tile + 1) * queries)
                query = qkv[half, rows, columns(place, 0)] * (mask * scale).astype(BF16)
                scores = matmul_right(key, query)
                probs = jnp.exp(scores - lse[index * 2 + part, :, rows])
                dprobs = matmul_right(value, dmixed[rows, here] * mask)
                inner = jnp.sum(dprobs * probs, axis=0, keepdims=True)
                probs_t[part, :, rows] = probs.astype(BF16)
                dscores_t[part, :, rows] = (probs * (dprobs - inner)).astype(BF16)
            query = qkv[half, :, columns(place, 0)] * (mask * scale).astype(BF16)
            terms = (
                matmul_left(dscores_t[part], key * mask),
                matmul(dscores_t[part], query),
                matmul(probs_t[part], dmixed[:, here] * mask),
            )
            if dquery is None:
                dquery, dkey, dvalue = terms
            else:
                dquery, dkey, dvalue = dquery + terms[0], dkey + terms[1], dvalue + terms[2]
        qkv[half, :, columns(place, 0)] = (dquery * scale).astype(BF16)
        qkv[half, :, columns(place, 1)] = dkey.astype(BF16)
        qkv[half, :, columns(place, 2)] = dvalue.astype(BF16)
        ticks(time + 2 * index, 2)
        return carry

    lax.fori_loop(0, 2 * pairs_half, attend_back, 0)
    time += 4 * pairs_half

    flip[...] = normed[...].T
    for half in (1, 0):
        target = held if half == 0 else other
        for part in range(3 * local // LANES):
            cols = slice(part * LANES, (part + 1) * LANES)
            grad = matmul(flip[...], qkv[half, :, cols])
            target[size.first_qkv + part] = grad.astype(BF16).reshape(SHARDS, ROWS, LANES)
        if half == 1:
            send_pairs(size.first_qkv, size.pieces - size.first_qkv)
    for half in range(2):
        table = vec if half == 0 else vec_other
        table[6:7, 0:local] = matmul(ones, qkv[half, :, 0:local])[0:1]
        table[6:7, local : 2 * local] = matmul(ones, qkv[half, :, 2 * local : 3 * local])[0:1]
    hidden[...] = matmul_right(qkv[0], wqkv[0])
    hidden[...] += matmul_right(qkv[1], wqkv[1])

    def first_back(tile, carry):
        sum_gain, sum_shift = carry
        rows = pl.ds(pl.multiple_of(tile * tiny, tiny), tiny)
        unit, rstd = norm_parts(x_s[rows].astype(F32))
        grad = hidden[rows]
        ffn[rows] = dn2[rows] + norm_back(grad * gain_attn[...], unit, rstd)
        return sum_gain + fold(grad * unit), sum_shift + fold(grad)

    sum_gain, sum_shift = lax.fori_loop(0, SEQ // tiny, first_back, (zero, zero))
    both(2, jnp.sum(sum_gain, axis=0, keepdims=True))
    both(3, jnp.sum(sum_shift, axis=0, keepdims=True))
    grad_copies = row_copies(ffn, out_grad, 1)
    for item in grad_copies:
        item.start()

    def vector_copy(step):
        if step == 0:
            source, partner = vec_other, {"tensor": 1 - core}
        else:
            bit = lax.rem(lax.div(me, 1 << (step - 1)), 2)
            source, partner = vec, {"dp": me + (1 - 2 * bit) * (1 << (step - 1))}
        return pltpu.make_async_remote_copy(
            src_ref=source,
            dst_ref=vec_landed.at[step],
            send_sem=vec_send.at[step],
            recv_sem=vec_recv.at[step],
            device_id=partner,
            device_id_type=MESH,
        )

    for step in range(bits + 1):
        vector_copy(step).start()
        ticks(time, 1)
        time += 1
        vector_copy(step).wait()
        vec[...] += vec_landed[step]
    vector_store = pltpu.make_async_copy(vec, out_vectors, row_sem.at[2])
    vector_store.start()
    ticks(time, pieces + LAG * sends - time)

    def finish(piece, carry):
        pair_copy(piece).wait_send()
        for step in range(bits, sends):
            copy(piece, step).wait_send()
        store(piece).wait()
        return carry

    lax.fori_loop(0, pieces, finish, 0)
    for item in gathers:
        item.wait_send()
    for local_copy, remote_copy in (result_copies, grad_copies):
        local_copy.wait()
        remote_copy.wait()
    vector_store.wait()


def run_layer(size, arrays, vectors):
    width, local, hidden = size.width, size.local, size.hidden
    rows = arrays[0].shape[0]
    steps = size.sends
    rank = pltpu.SemaphoreType
    any_space = pl.BlockSpec(memory_space=pl.ANY)
    in_vmem = pl.BlockSpec(memory_space=pltpu.VMEM)
    piece_shape = (size.pieces, SHARDS, ROWS, LANES)
    scratch = [
        pltpu.VMEM((2, width, 3 * local), BF16),
        pltpu.VMEM((2 * local, width), BF16),
        pltpu.VMEM((2, width, hidden), BF16),
        pltpu.VMEM((2, hidden, width), BF16),
        pltpu.VMEM((1, local), F32),
        pltpu.VMEM((1, local), F32),
        pltpu.VMEM((1, hidden), F32),
        pltpu.VMEM((SEQ, width), BF16),
        pltpu.VMEM((SEQ, width), BF16),
        pltpu.VMEM((SEQ, width), BF16),
        pltpu.VMEM((2, SEQ, 3 * local), BF16),
        pltpu.VMEM((SEQ, width), BF16),
        pltpu.VMEM((2 * local // HEAD, 1, SEQ), F32),
        pltpu.VMEM((SEQ, width), F32),
        pltpu.VMEM((SEQ, width), BF16),
        pltpu.VMEM((width, SEQ), BF16),
        pltpu.VMEM((SEQ, width), F32),
        pltpu.VMEM((SEQ, width), F32),
        pltpu.VMEM((SEQ, width), BF16),
        pltpu.VMEM((SEQ, width), BF16),
        pltpu.VMEM((width, SEQ), BF16),
        pltpu.VMEM((256, width), F32),
        pltpu.VMEM((256, width), F32),
        pltpu.VMEM((SEQ, width), BF16),
        pltpu.VMEM((SEQ, width), BF16),
        pltpu.VMEM((SEQ, width), BF16),
        pltpu.VMEM((LANES // HEAD, SEQ, SEQ), BF16),
        pltpu.VMEM((LANES // HEAD, SEQ, SEQ), BF16),
        pltpu.VMEM(piece_shape, BF16),
        pltpu.VMEM(piece_shape, BF16),
        pltpu.VMEM(piece_shape, BF16),
        pltpu.VMEM((size.pieces, size.landing, ROWS, LANES), BF16),
        pltpu.VMEM((16, width), F32),
        pltpu.VMEM((16, width), F32),
        pltpu.VMEM((size.bits + 1, 16, width), F32),
        rank.DMA((8,)),
        rank.DMA((9,)),
        rank.DMA((9,)),
        rank.DMA((size.pieces,)),
        rank.DMA((size.pieces,)),
        rank.DMA((size.pieces, steps)),
        rank.DMA((size.pieces, steps)),
        rank.REGULAR((size.pieces, size.halving)),
        rank.DMA((size.pieces,)),
        rank.DMA((size.bits + 1,)),
        rank.DMA((size.bits + 1,)),
        rank.DMA((2,)),
        rank.DMA((2,)),
        rank.DMA((3,)),
    ]
    return pl.pallas_call(
        functools.partial(layer_kernel, size),
        out_shape=(
            jax.ShapeDtypeStruct((rows, width), BF16),
            jax.ShapeDtypeStruct((rows, width), F32),
            jax.ShapeDtypeStruct(piece_shape, BF16),
            jax.ShapeDtypeStruct((16, width), F32),
        ),
        in_specs=[any_space] * len(arrays) + [in_vmem] * len(vectors),
        out_specs=(any_space,) * 4,
        scratch_shapes=scratch,
        compiler_params=pltpu.CompilerParams(
            collective_id=0, has_side_effects=True, vmem_limit_bytes=67043328
        ),
        name="layer",
    )(*arrays, *vectors)


def unpack_kernel(size, pieces, vectors, *refs):
    g_wq, g_wk, g_wv, g_wo, g_wi, g_wb = refs[:6]
    rows_out = refs[6:15]
    held, s_in, s_back, s_qkv, s_out, sem, out_sem = refs[15:]
    width, local = size.width, size.local
    wide = 2 * LANES
    half_rows = ROWS * SHARDS // 2
    spans = []
    for chunk in range(size.chunks):
        first = chunk * size.per_chunk
        spans.append((first, size.block))
        spans.append((first + size.block, size.block))
    spans.append((size.first_out, size.first_qkv - size.first_out))
    for index in range(3):
        spans.append((size.first_qkv + index * local // LANES, local // LANES))
    copies = []
    for index, (first, amount) in enumerate(spans):
        item = pltpu.make_async_copy(
            pieces.at[pl.ds(first, amount)], held.at[pl.ds(first, amount)], sem.at[index]
        )
        item.start()
        copies.append(item)
    for ref, row, begin, amount in zip(
        rows_out,
        (6, 6, 0, 7, 1, 2, 3, 4, 5),
        (0, local, 0, 0, 0, 0, 0, 0, 0),
        (local, local, width, width, width, width, width, width, width),
    ):
        for chunk in range(ref.shape[1] // amount):
            ref[:, chunk * amount : (chunk + 1) * amount] = vectors[
                row + chunk : row + chunk + 1, begin : begin + amount
            ]

    outs = []

    def put(source, target):
        item = pltpu.make_async_copy(source, target, out_sem.at[len(outs)])
        item.start()
        outs.append(item)

    def columns(first, amount, target, begin):
        for index in range(amount):
            target[:, begin + index * LANES : begin + (index + 1) * LANES] = (
                held[first + index].reshape(SHARDS * ROWS, LANES).astype(F32)
            )

    def blocks(first, rows, target, begin):
        for block in range(rows // half_rows):
            for part in range(width // wide):
                for side in range(2):
                    value = held[
                        first + block * (width // wide) + part,
                        side * (SHARDS // 2) : (side + 1) * (SHARDS // 2),
                    ]
                    target[
                        begin + block * half_rows : begin + (block + 1) * half_rows,
                        part * wide + side * LANES : part * wide + (side + 1) * LANES,
                    ] = value.reshape(half_rows, LANES).astype(F32)

    at = 0
    for chunk in range(size.chunks):
        first = chunk * size.per_chunk
        copies[at].wait()
        columns(first, size.block, s_in.at[chunk], 0)
        put(s_in.at[chunk], g_wi.at[:, pl.ds(chunk * width, width)])
        copies[at + 1].wait()
        blocks(first + size.block, width, s_back, chunk * width)
        put(
            s_back.at[pl.ds(chunk * width, width)],
            g_wb.at[pl.ds(chunk * width, width)],
        )
        at += 2
    copies[at].wait()
    blocks(size.first_out, local, s_out, 0)
    put(s_out, g_wo)
    at += 1
    for index, target in enumerate((g_wq, g_wk, g_wv)):
        copies[at].wait()
        columns(size.first_qkv + index * local // LANES, local // LANES, s_qkv.at[index], 0)
        put(s_qkv.at[index], target)
        at += 1
    for item in outs:
        item.wait()


def unpack(size, pieces, vectors):
    width, local, hidden = size.width, size.local, size.hidden
    any_space = pl.BlockSpec(memory_space=pl.ANY)
    in_vmem = pl.BlockSpec(memory_space=pltpu.VMEM)
    matrices = [(width, local)] * 3 + [(local, width), (width, hidden), (hidden, width)]
    rows = [local, local, width, hidden, width, width, width, width, width]
    transfers = 2 * size.chunks + 4
    return pl.pallas_call(
        functools.partial(unpack_kernel, size),
        out_shape=tuple(jax.ShapeDtypeStruct(shape, F32) for shape in matrices)
        + tuple(jax.ShapeDtypeStruct((1, amount), F32) for amount in rows),
        in_specs=[any_space, in_vmem],
        out_specs=(any_space,) * 6 + (in_vmem,) * 9,
        scratch_shapes=[
            pltpu.VMEM(pieces.shape, BF16),
            pltpu.VMEM((size.chunks, width, width), F32),
            pltpu.VMEM((hidden, width), F32),
            pltpu.VMEM((3, width, local), F32),
            pltpu.VMEM((local, width), F32),
            pltpu.SemaphoreType.DMA((transfers,)),
            pltpu.SemaphoreType.DMA((transfers,)),
        ],
        compiler_params=pltpu.CompilerParams(vmem_limit_bytes=48 << 20),
        name="unpack",
    )(pieces, vectors)


def on_device(
    tokens,
    cotangent,
    w_query,
    b_query,
    w_key,
    w_value,
    b_value,
    w_out,
    b_out,
    w_in,
    b_in,
    w_back,
    b_back,
    gain_attn,
    shift_attn,
    gain_ffn,
    shift_ffn,
):
    size = Sizes(lax.axis_size("dp"), tokens, w_query, w_in)
    assert tokens.shape[0] == SEQ * lax.axis_size("tensor") and lax.axis_size("tensor") == 2
    assert size.count == 1 << size.bits and size.width == SHARDS * ROWS
    vectors = (
        b_query,
        b_value,
        b_out,
        b_in,
        b_back,
        gain_attn,
        shift_attn,
        gain_ffn,
        shift_ffn,
    )
    rows, grad_rows, pieces, sums = run_layer(
        size,
        (tokens, cotangent, w_query, w_key, w_value, w_out, w_in, w_back),
        tuple(item.reshape(1, -1) for item in vectors),
    )
    outs = unpack(size, pieces, sums)
    g_wq, g_wk, g_wv, g_wo, g_wi, g_wb = outs[:6]
    g_bq, g_bv, g_bo, g_bi, g_bb, g_ga, g_sa, g_gf, g_sf = (item.reshape(-1) for item in outs[6:])
    return (
        rows,
        grad_rows,
        g_wq,
        g_bq,
        g_wk,
        g_wv,
        g_bv,
        g_wo,
        g_bo,
        g_wi,
        g_bi,
        g_wb,
        g_bb,
        g_ga,
        g_sa,
        g_gf,
        g_sf,
    )


def solution(mesh):
    columns, rows, vector, whole = P(None, "tensor"), P("tensor", None), P("tensor"), P()
    weights = (
        columns,
        vector,
        columns,
        columns,
        vector,
        rows,
        whole,
        columns,
        vector,
        rows,
        whole,
        whole,
        whole,
        whole,
        whole,
    )
    data = (P("dp", None), P("dp", None))
    return jax.shard_map(
        on_device, mesh=mesh, in_specs=data + weights, out_specs=data + weights, check_vma=False
    )
```

time: 1350 us -> 224 us (0.17)
  blocking collectives: 612 us -> 0 us
  local copies, waits for them, and re-layouts: 276 us -> 16.3 us
  waiting for transfers between devices: 252 us -> 0 us
  Pallas kernels: 0 us -> 201 us
  matrix products: 107 us -> 0 us
  other arithmetic: 76.4 us -> 5.44 us
  between operations: 16.8 us -> 0.69 us
    unnamed x1 -> x0, blocking collectives: 587 us -> none
    unnamed x2 -> x0, waiting for transfers between devices: 232 us -> none
    pallas_call x0 -> x2, Pallas kernels: none -> 201 us  [the longest x1 194 us: run_layer(): pl.pallas_call(functools.partial(layer_kernel, size), out_shape=(jax.Shap...]
    while x260 -> x0, local copies, waits for them, and re-layouts: 193 us -> none
    dot_general x48 -> x0, matrix products: 107 us -> none  [the longest x12 33.9 us: matmul(): return jnp.dot(left, right, preferred_element_type=jnp.float32)]
    reshape x13 -> x9, local copies, waits for them, and re-layouts: 40.7 us -> 11.4 us  [on_device(): item.reshape(1, -1)]
    add x4 -> x0, other arithmetic: 25.7 us -> none  [the longest x2 25.7 us: stepper(): updated = carry + flat]
    reduce_sum x18 -> x0, other arithmetic: 25.1 us -> none  [the longest x2 6.31 us: one_batch(): part_gain_ffn = jnp.sum(dnormed2 * unit_two, axis=0)]
  transfers between devices with their start and end apart: 9 -> 0, of which waited for: 3 -> 0; matrix products, arithmetic and copies ran while one was open for 20% -> 0% of each run, Pallas kernels for 0% -> 0%
where the time goes in v2:
time: 224 us
  Pallas kernels  201 us (90%)
  local copies, waits for them, and re-layouts  16.3 us (7%)
  other arithmetic  5.44 us (2%)
    pallas_call x1, Pallas kernels, run_layer(): pl.pallas_call(functools.partial(layer_kernel, size), out_shape=(jax.Shap...  194 us
    reshape x9, local copies, waits for them, and re-layouts, on_device(): item.reshape(1, -1)  11.4 us
    pallas_call x1, Pallas kernels, unpack(): pl.pallas_call(functools.partial(unpack_kernel, size), out_shape=tuple((j...  7.33 us
    pallas_call x9, other arithmetic, unpack(): pl.pallas_call(functools.partial(unpack_kernel, size), out_shape=tuple((j...  5.44 us
    unnamed x8, local copies, waits for them, and re-layouts  4.92 us

profile of v2, /device:TPU:0, one launch (start us, length us, event | category | flops | bytes accessed | tf_op | source)
XLA Modules:
  0.0 223.7 jit_solution(14883140890810517426)
XLA Ops:
  0.7 1.2 reshape.88.b_query
  1.9 1.2 reshape.89.b_value
  3.1 1.3 reshape.90.b_out
  4.4 1.3 reshape.92.b_back
  5.7 1.3 reshape.93.gain_attn
  6.9 1.3 reshape.94.shift_attn
  8.2 1.3 reshape.95.gain_ffn
  9.5 1.3 reshape.96.shift_ffn
  10.7 1.3 reshape.91.b_in
  12.0 193.9 %layer.1 = (bf16[1024,768]{1,0:T(8,128)(2,1)}, f32[1024,768]{1,0:T(8,128)}, bf16[36,16,48,128]{3,2,1,0:T(8,128)(2,1)}, f32[16,768]{1,0:T(8,128)}) custom-call(bf16[1024,768]{1,0:T(8,128)(2,1)} %tokens.1, bf16[1024,768]{1,0:T(8,128)(2,1)} %cotangent.1, bf16[768,384]{1,0:T(8,128)(2,1)} %w_query.1, bf16[768,384]{1,0:T(8,128)(2,1)} %w_key.1, ...), custom_call_target="tpu_custom_call" | custom-call | tf_op jit(solution)/shard_map/layer/pallas_call | solution.py:745
  206.0 0.8 copy-done
  206.8 7.3 %unpack.1 = (f32[768,384]{1,0:T(8,128)}, f32[768,384]{1,0:T(8,128)}, f32[768,384]{1,0:T(8,128)}, f32[384,768]{1,0:T(8,128)}, f32[768,1536]{1,0:T(8,128)}, /*inde...) custom-call(bf16[36,16,48,128]{3,2,1,0:T(8,128)(2,1)} %get-tuple-ele, ...), custom_call_target="tpu_custom_call" | custom-call | tf_op jit(solution)/shard_map/unpack/pallas_call | solution.py:855
  214.1 0.6 reduce
  214.7 0.6 reduce.1
  215.3 0.6 reduce.2
  215.9 0.6 reduce.4
  216.5 0.6 reduce.5
  217.1 0.6 reduce.6
  217.7 0.6 reduce.7
  218.3 0.6 reduce.8
  218.9 0.6 reduce.3
  219.6 1.1 copy.36
  220.7 1.3 copy-done.1
  222.0 1.7 copy.37
  (4 shorter events, 0.0 us)
Async XLA Ops:
  206.0 0.8 copy-start
  206.8 12.8 %copy-start.2 = (bf16[1024,768]{1,0:T(8,128)(2,1)S(1)}, bf16[1024,768]{1,0:T(8,128)(2,1)}, u32[]{:S(2)}) copy-start(bf16[1024,768]{1,0:T(8,128)(2,1)} %get-tuple-element.72) | copy-start | bytes 4718596
  219.6 2.5 %copy-start.1 = (f32[1024,768]{1,0:T(8,128)S(1)}, f32[1024,768]{1,0:T(8,128)}, u32[]{:S(2)}) copy-start(f32[1024,768]{1,0:T(8,128)} %get-tuple-element.73) | copy-start | bytes 9437188

commit v3 on v2

--- a/solution.py
+++ b/solution.py
@@ -14,6 +14,7 @@
 ROWS = 48
 LANES = 128
 LAG = 2
+DELAY = 0
 MESH = pl.DeviceIdType.MESH
 F32 = jnp.float32
 BF16 = jnp.bfloat16
@@ -44,6 +45,10 @@
         - jnp.mean(scaled, axis=-1, keepdims=True)
         - unit * jnp.mean(scaled * unit, axis=-1, keepdims=True)
     )
+
+
+def row_of(ref):
+    return ref[...].reshape(1, -1)
 
 
 def fold(value):
@@ -141,7 +146,6 @@
     pair_recv,
     send_sem,
     recv_sem,
-    free_sem,
     store_sem,
     vec_send,
     vec_recv,
@@ -168,10 +172,6 @@
         )
         return stride, lax.rem(lax.div(me, stride), 2)
 
-    def partner_of(colour, level):
-        stride, bit = bit_at(colour, level)
-        return me + (1 - 2 * bit) * stride
-
     def base_of(colour, level):
         base = 0
         for earlier in range(min(level, halving)):
@@ -197,10 +197,12 @@
         else:
             half = SHARDS >> halving
             start = base
-        source = held.at[piece, pl.ds(start, half)]
-        target = source
         if step < bits:
+            source = held.at[piece, pl.ds(start, half)]
             target = landed.at[piece, pl.ds(landing_of(level)[0], half)]
+        else:
+            source = pair.at[piece, pl.ds(start, half)]
+            target = source
         return pltpu.make_async_remote_copy(
             src_ref=source,
             dst_ref=target,
@@ -214,14 +216,16 @@
         colour = colour_of(piece)
         base = base_of(colour, level + 1)
         place, half = landing_of(level)
-
-        def one(shard, carry):
-            mine = held[piece, base + shard].astype(F32)
-            theirs = landed[piece, place + shard].astype(F32)
-            held[piece, base + shard] = (mine + theirs).astype(BF16)
+        total = held if level < bits - 1 else pair
+        group = min(half, 4)
+
+        def some(index, carry):
+            mine = held[piece, pl.ds(base + index * group, group)]
+            theirs = landed[piece, pl.ds(place + index * group, group)]
+            total[piece, pl.ds(base + index * group, group)] = mine + theirs
             return carry
 
-        lax.fori_loop(0, half, one, 0)
+        lax.fori_loop(0, half // group, some, 0)
 
     def pair_copy(piece):
         return pltpu.make_async_remote_copy(
@@ -234,40 +238,39 @@
         )
 
     def store(piece):
-        return pltpu.make_async_copy(held.at[piece], out_pieces.at[piece], store_sem.at[piece])
+        return pltpu.make_async_copy(pair.at[piece], out_pieces.at[piece], store_sem.at[piece])
 
     def advance(piece, step):
         if step == 0:
             pair_copy(piece).wait_recv()
 
-            def one(shard, carry):
-                mine = held[piece, shard].astype(F32)
-                held[piece, shard] = (mine + pair[piece, shard].astype(F32)).astype(BF16)
+            def some(index, carry):
+                shards = pl.ds(index * 4, 4)
+                held[piece, shards] = held[piece, shards] + pair[piece, shards]
                 return carry
 
-            lax.fori_loop(0, SHARDS, one, 0)
+            lax.fori_loop(0, SHARDS // 4, some, 0)
         else:
             copy(piece, step - 1).wait_recv()
+            if halving < step <= bits:
+                copy(piece, step - 1).wait_send()
             if step <= bits:
-                copy(piece, step - 1).wait_send()
-                if step <= halving:
-                    pl.semaphore_signal(
-                        free_sem.at[piece, step - 1],
-                        inc=1,
-                        device_id={"dp": partner_of(colour_of(piece), step - 1)},
-                        device_id_type=MESH,
-                    )
                 add_level(piece, step - 1)
         if step < sends:
-            if step >= bits:
-                pl.semaphore_wait(free_sem.at[piece, level_of(step)], 1)
             copy(piece, step).start()
         else:
             store(piece).start()
+            for earlier in early_sends:
+                copy(piece, earlier).wait_send()
+
+    early_sends = range(halving)
+
+    def offset_of(step):
+        return LAG * step + (DELAY if step >= bits else 0)
 
     def tick(time, carry):
         for step in range(sends + 1):
-            piece = time - LAG * step
+            piece = time - offset_of(step)
 
             @pl.when((piece >= 0) & (piece < pieces))
             def _():
@@ -342,13 +345,13 @@
     ffn[...] = jnp.zeros_like(ffn)
     dn2[...] = jnp.zeros_like(dn2)
 
-    small = 64
+    small = 128
     loads[0].wait()
 
     def first_norm(tile, carry):
         rows = pl.ds(pl.multiple_of(tile * small, small), small)
         unit, rstd = norm_parts(x_s[rows].astype(F32))
-        normed[rows] = (unit * gain_attn[...] + shift_attn[...]).astype(BF16)
+        normed[rows] = (unit * row_of(gain_attn) + row_of(shift_attn)).astype(BF16)
         return carry
 
     lax.fori_loop(0, SEQ // small, first_norm, 0)
@@ -363,13 +366,13 @@
                 item.wait_recv()
             bias_query, bias_value = bias_q, bias_v
         qkv[half, :, 0:local] = (
-            matmul(normed[...], wqkv[half, :, 0:local]) + bias_query[...]
+            matmul(normed[...], wqkv[half, :, 0:local]) + row_of(bias_query)
         ).astype(BF16)
         qkv[half, :, local : 2 * local] = matmul(
             normed[...], wqkv[half, :, local : 2 * local]
         ).astype(BF16)
         qkv[half, :, 2 * local : 3 * local] = (
-            matmul(normed[...], wqkv[half, :, 2 * local : 3 * local]) + bias_value[...]
+            matmul(normed[...], wqkv[half, :, 2 * local : 3 * local]) + row_of(bias_value)
         ).astype(BF16)
 
     pairs_half = local // LANES
@@ -412,10 +415,10 @@
 
     def second_norm(tile, carry):
         rows = pl.ds(pl.multiple_of(tile * small, small), small)
-        whole = x_s[rows].astype(F32) + (hidden[rows] + b_out[...])
+        whole = x_s[rows].astype(F32) + (hidden[rows] + row_of(b_out))
         hidden[rows] = whole
         unit, rstd = norm_parts(whole)
-        normed2[rows] = (unit * gain_ffn[...] + shift_ffn[...]).astype(BF16)
+        normed2[rows] = (unit * row_of(gain_ffn) + row_of(shift_ffn)).astype(BF16)
         return carry
 
     lax.fori_loop(0, SEQ // small, second_norm, 0)
@@ -469,7 +472,7 @@
             def inner(step, carry):
                 piece = pl.ds(pl.multiple_of(step * fine, fine), fine)
                 there = pl.ds(pl.multiple_of(tile * tall + step * fine, fine), fine)
-                pre = wide_a[piece] + bias_row[:, units]
+                pre = wide_a[piece] + bias_row[units].reshape(1, -1)
                 phi = 0.5 * (1.0 + lax.erf(pre * 0.7071067811865476))
                 act[there] = (pre * phi).astype(BF16)
                 slope = phi + pre * jnp.exp(-0.5 * pre * pre) * 0.3989422804014327
@@ -480,49 +483,52 @@
             return carry
 
         lax.fori_loop(0, SEQ // tall, rows_tile, 0)
+        flip[...] = act[...].T
         slots(0)
-        flip[...] = act[...].T
-        ffn[...] += matmul(act[...], wb[half, units, :])
-        slots(1)
-        dn2[...] += matmul_right(dpre[...], wi[half, :, units])
-        slots(2)
         for part in range(width // 256):
             cols = slice(part * 256, (part + 1) * 256)
             hand_in(target, first, matmul(flip2[...], dpre[:, cols]), "in", part)
-        slots(3)
         for part in range(width // 256):
             cols = slice(part * 256, (part + 1) * 256)
             hand_in(target, first + size.block, matmul(flip[...], dy_s[:, cols]), "out", part)
-        slots(4)
+        slots(1)
+        ffn[...] += matmul(act[...], wb[half, units, :])
+        dn2[...] += matmul_right(dpre[...], wi[half, :, units])
         sums = matmul(ones, dpre[...])[0:1]
         (vec if half == 0 else vec_other)[pl.ds(7 + chunk, 1)] = sums
 
     def feed_both(chunk, carry):
-        def slots(offset):
+        def slots(offset, half):
             def place(index):
-                first = (chunk - 1) * 10 + offset + index
-                lax.fori_loop(first, jnp.where(chunk > 0, first + 1, first), tick, 0)
+                if index == 0:
+                    first = 1 + (chunk - 1) * 4 + offset
+                    lax.fori_loop(first, jnp.where(chunk > 0, first + 1, first), tick, 0)
+                elif half == 1:
+                    send_pairs(chunk * size.per_chunk, size.per_chunk)
+                    first = 2 + (chunk - 1) * 4
+                    lax.fori_loop(first, jnp.where(chunk > 0, first + 1, first), tick, 0)
+                else:
+                    ticks(chunk * 4, 1)
 
             return place
 
-        feed(chunk, 1, slots(0))
-        send_pairs(chunk * size.per_chunk, size.per_chunk)
-        feed(chunk, 0, slots(5))
+        feed(chunk, 1, slots(0, 1))
+        feed(chunk, 0, slots(2, 0))
         return carry
 
     lax.fori_loop(0, size.chunks, feed_both, 0)
-    time = 10 * (size.chunks - 1)
-
-    tiny = 32
+    time = 4 * size.chunks - 3
+
+    tiny = 64
 
     def second_back(tile, carry):
         sum_gain, sum_shift, sum_out = carry
         rows = pl.ds(pl.multiple_of(tile * tiny, tiny), tiny)
         whole = hidden[rows]
-        result[rows] = (whole + (ffn[rows] + b_back[...])).astype(BF16)
+        result[rows] = (whole + (ffn[rows] + row_of(b_back))).astype(BF16)
         unit, rstd = norm_parts(whole)
         grad = dn2[rows]
-        dhidden = dy_s[rows].astype(F32) + norm_back(grad * gain_ffn[...], unit, rstd)
+        dhidden = dy_s[rows].astype(F32) + norm_back(grad * row_of(gain_ffn), unit, rstd)
         dn2[rows] = dhidden
         rounded = dhidden.astype(BF16)
         dattn[rows] = rounded
@@ -562,8 +568,8 @@
     result_copies = row_copies(result, out_rows, 0)
     for item in result_copies:
         item.start()
-    ticks(time, 2)
-    time += 2
+    ticks(time, 1)
+    time += 1
 
     flip[...] = mixed[...].T
     for part in range(width // 256):
@@ -605,11 +611,11 @@
         qkv[half, :, columns(place, 0)] = (dquery * scale).astype(BF16)
         qkv[half, :, columns(place, 1)] = dkey.astype(BF16)
         qkv[half, :, columns(place, 2)] = dvalue.astype(BF16)
-        ticks(time + 2 * index, 2)
+        ticks(time + index, 1)
         return carry
 
     lax.fori_loop(0, 2 * pairs_half, attend_back, 0)
-    time += 4 * pairs_half
+    time += 2 * pairs_half
 
     flip[...] = normed[...].T
     for half in (1, 0):
@@ -620,19 +626,23 @@
             target[size.first_qkv + part] = grad.astype(BF16).reshape(SHARDS, ROWS, LANES)
         if half == 1:
             send_pairs(size.first_qkv, size.pieces - size.first_qkv)
+        ticks(time, 1)
+        time += 1
     for half in range(2):
         table = vec if half == 0 else vec_other
         table[6:7, 0:local] = matmul(ones, qkv[half, :, 0:local])[0:1]
         table[6:7, local : 2 * local] = matmul(ones, qkv[half, :, 2 * local : 3 * local])[0:1]
     hidden[...] = matmul_right(qkv[0], wqkv[0])
     hidden[...] += matmul_right(qkv[1], wqkv[1])
+    ticks(time, 1)
+    time += 1
 
     def first_back(tile, carry):
         sum_gain, sum_shift = carry
         rows = pl.ds(pl.multiple_of(tile * tiny, tiny), tiny)
         unit, rstd = norm_parts(x_s[rows].astype(F32))
         grad = hidden[rows]
-        ffn[rows] = dn2[rows] + norm_back(grad * gain_attn[...], unit, rstd)
+        ffn[rows] = dn2[rows] + norm_back(grad * row_of(gain_attn), unit, rstd)
         return sum_gain + fold(grad * unit), sum_shift + fold(grad)
 
     sum_gain, sum_shift = lax.fori_loop(0, SEQ // tiny, first_back, (zero, zero))
@@ -659,13 +669,13 @@
 
     for step in range(bits + 1):
         vector_copy(step).start()
-        ticks(time, 1)
-        time += 1
+        ticks(time, 3)
+        time += 3
         vector_copy(step).wait()
         vec[...] += vec_landed[step]
     vector_store = pltpu.make_async_copy(vec, out_vectors, row_sem.at[2])
     vector_store.start()
-    ticks(time, pieces + LAG * sends - time)
+    ticks(time, pieces + offset_of(sends) - time)
 
     def finish(piece, carry):
         pair_copy(piece).wait_send()
@@ -696,9 +706,9 @@
         pltpu.VMEM((2 * local, width), BF16),
         pltpu.VMEM((2, width, hidden), BF16),
         pltpu.VMEM((2, hidden, width), BF16),
-        pltpu.VMEM((1, local), F32),
-        pltpu.VMEM((1, local), F32),
-        pltpu.VMEM((1, hidden), F32),
+        pltpu.VMEM((local,), F32),
+        pltpu.VMEM((local,), F32),
+        pltpu.VMEM((hidden,), F32),
         pltpu.VMEM((SEQ, width), BF16),
         pltpu.VMEM((SEQ, width), BF16),
         pltpu.VMEM((SEQ, width), BF16),
@@ -734,7 +744,6 @@
         rank.DMA((size.pieces,)),
         rank.DMA((size.pieces, steps)),
         rank.DMA((size.pieces, steps)),
-        rank.REGULAR((size.pieces, size.halving)),
         rank.DMA((size.pieces,)),
         rank.DMA((size.bits + 1,)),
         rank.DMA((size.bits + 1,)),
@@ -760,10 +769,10 @@
     )(*arrays, *vectors)
 
 
-def unpack_kernel(size, pieces, vectors, *refs):
-    g_wq, g_wk, g_wv, g_wo, g_wi, g_wb = refs[:6]
-    rows_out = refs[6:15]
-    held, s_in, s_back, s_qkv, s_out, sem, out_sem = refs[15:]
+def unpack_kernel(size, pieces, vectors_in, rows_in, grad_in, *refs):
+    g_wq, g_wk, g_wv, g_wo, g_wi, g_wb, rows_end, grad_end = refs[:8]
+    rows_out = refs[8:17]
+    held, s_in, s_back, s_qkv, s_out, vectors, rows, grad, sem, out_sem, side_sem = refs[17:]
     width, local = size.width, size.local
     wide = 2 * LANES
     half_rows = ROWS * SHARDS // 2
@@ -782,15 +791,24 @@
         )
         item.start()
         copies.append(item)
+    sides = [
+        pltpu.make_async_copy(source, target, side_sem.at[index])
+        for index, (source, target) in enumerate(
+            ((vectors_in, vectors), (rows_in, rows), (grad_in, grad))
+        )
+    ]
+    for item in sides:
+        item.start()
+    sides[0].wait()
     for ref, row, begin, amount in zip(
         rows_out,
         (6, 6, 0, 7, 1, 2, 3, 4, 5),
         (0, local, 0, 0, 0, 0, 0, 0, 0),
         (local, local, width, width, width, width, width, width, width),
     ):
-        for chunk in range(ref.shape[1] // amount):
-            ref[:, chunk * amount : (chunk + 1) * amount] = vectors[
-                row + chunk : row + chunk + 1, begin : begin + amount
+        for chunk in range(ref.shape[0] // amount):
+            ref[chunk * amount : (chunk + 1) * amount] = vectors[
+                row + chunk, begin : begin + amount
             ]
 
     outs = []
@@ -841,35 +859,44 @@
         columns(size.first_qkv + index * local // LANES, local // LANES, s_qkv.at[index], 0)
         put(s_qkv.at[index], target)
         at += 1
+    sides[1].wait()
+    put(rows, rows_end)
+    sides[2].wait()
+    put(grad, grad_end)
     for item in outs:
         item.wait()
 
 
-def unpack(size, pieces, vectors):
+def unpack(size, pieces, vectors, block_rows, grad_rows):
     width, local, hidden = size.width, size.local, size.hidden
     any_space = pl.BlockSpec(memory_space=pl.ANY)
     in_vmem = pl.BlockSpec(memory_space=pltpu.VMEM)
     matrices = [(width, local)] * 3 + [(local, width), (width, hidden), (hidden, width)]
     rows = [local, local, width, hidden, width, width, width, width, width]
-    transfers = 2 * size.chunks + 4
+    transfers = 2 * size.chunks + 6
     return pl.pallas_call(
         functools.partial(unpack_kernel, size),
         out_shape=tuple(jax.ShapeDtypeStruct(shape, F32) for shape in matrices)
-        + tuple(jax.ShapeDtypeStruct((1, amount), F32) for amount in rows),
-        in_specs=[any_space, in_vmem],
-        out_specs=(any_space,) * 6 + (in_vmem,) * 9,
+        + tuple(jax.ShapeDtypeStruct(item.shape, item.dtype) for item in (block_rows, grad_rows))
+        + tuple(jax.ShapeDtypeStruct((amount,), F32) for amount in rows),
+        in_specs=[any_space] * 4,
+        out_specs=(any_space,) * 8 + (in_vmem,) * 9,
         scratch_shapes=[
             pltpu.VMEM(pieces.shape, BF16),
             pltpu.VMEM((size.chunks, width, width), F32),
             pltpu.VMEM((hidden, width), F32),
             pltpu.VMEM((3, width, local), F32),
             pltpu.VMEM((local, width), F32),
+            pltpu.VMEM(vectors.shape, F32),
+            pltpu.VMEM(block_rows.shape, BF16),
+            pltpu.VMEM(grad_rows.shape, F32),
             pltpu.SemaphoreType.DMA((transfers,)),
             pltpu.SemaphoreType.DMA((transfers,)),
+            pltpu.SemaphoreType.DMA((3,)),
         ],
         compiler_params=pltpu.CompilerParams(vmem_limit_bytes=48 << 20),
         name="unpack",
-    )(pieces, vectors)
+    )(pieces, vectors, block_rows, grad_rows)
 
 
 def on_device(
@@ -908,14 +935,13 @@
     rows, grad_rows, pieces, sums = run_layer(
         size,
         (tokens, cotangent, w_query, w_key, w_value, w_out, w_in, w_back),
-        tuple(item.reshape(1, -1) for item in vectors),
+        vectors,
     )
-    outs = unpack(size, pieces, sums)
+    outs = unpack(size, pieces, sums, rows, grad_rows)
     g_wq, g_wk, g_wv, g_wo, g_wi, g_wb = outs[:6]
-    g_bq, g_bv, g_bo, g_bi, g_bb, g_ga, g_sa, g_gf, g_sf = (item.reshape(-1) for item in outs[6:])
+    g_bq, g_bv, g_bo, g_bi, g_bb, g_ga, g_sa, g_gf, g_sf = outs[8:]
     return (
-        rows,
-        grad_rows,
+        *outs[6:8],
         g_wq,
         g_bq,
         g_wk,

time: 224 us -> 185 us (0.83)
  Pallas kernels: 201 us -> 180 us
  local copies, waits for them, and re-layouts: 16.3 us -> 4.09 us
  other arithmetic: 5.44 us -> 0 us
    pallas_call x1, Pallas kernels: 194 us -> 171 us  [run_layer(): pl.pallas_call(functools.partial(layer_kernel, size), out_shape=(jax.Shap...]
    reshape x9 -> x0, local copies, waits for them, and re-layouts: 11.4 us -> none  [on_device(): item.reshape(1, -1)]
    pallas_call x9 -> x0, other arithmetic: 5.44 us -> none  [unpack(): pl.pallas_call(functools.partial(unpack_kernel, size), out_shape=tuple((j...]
    unnamed x8 -> x6, local copies, waits for them, and re-layouts: 4.92 us -> 4.09 us
where the time goes in v3:
time: 185 us
  Pallas kernels  180 us (97%)
  local copies, waits for them, and re-layouts  4.09 us (2%)
    pallas_call x1, Pallas kernels, run_layer(): pl.pallas_call(functools.partial(layer_kernel, size), out_shape=(jax.Shap...  171 us
    pallas_call x1, Pallas kernels, unpack(): pl.pallas_call(functools.partial(unpack_kernel, size), out_shape=tuple((j...  8.87 us
    unnamed x6, local copies, waits for them, and re-layouts  4.09 us

profile of v3, /device:TPU:0, one launch (start us, length us, event | category | flops | bytes accessed | tf_op | source)
XLA Modules:
  0.0 184.6 jit_solution(439169338934653060)
XLA Ops:
  0.7 170.7 %layer.1 = (bf16[1024,768]{1,0:T(8,128)(2,1)}, f32[1024,768]{1,0:T(8,128)}, bf16[36,16,48,128]{3,2,1,0:T(8,128)(2,1)}, f32[16,768]{1,0:T(8,128)}) custom-call(bf16[1024,768]{1,0:T(8,128)(2,1)} %tokens.1, bf16[1024,768]{1,0:T(8,128)(2,1)} %cotangent.1, bf16[768,384]{1,0:T(8,128)(2,1)} %w_query.1, bf16[768,384]{1,0:T(8,128)(2,1)} %w_key.1, ...), custom_call_target="tpu_custom_call" | custom-call | tf_op jit(solution)/shard_map/layer/pallas_call | solution.py:754
  171.4 0.0 copy-start
  171.4 1.9 %copy-done = f32[1024,768]{1,0:T(8,128)S(1)} copy-done((f32[1024,768]{1,0:T(8,128)S(1)}, f32[1024,768]{1,0:T(8,128)}, u32[]{:S(2)}) %copy-start) | copy-done | bytes 3145752
  173.3 0.0 copy-start.1
  173.3 1.4 copy-done.1
  174.7 0.0 copy-start.2
  174.7 0.8 copy-done.2
  175.5 8.9 %unpack.1 = (f32[768,384]{1,0:T(8,128)}, f32[768,384]{1,0:T(8,128)}, f32[768,384]{1,0:T(8,128)}, f32[384,768]{1,0:T(8,128)}, f32[768,1536]{1,0:T(8,128)}, /*inde...) custom-call(bf16[36,16,48,128]{3,2,1,0:T(8,128)(2,1)} %get-tuple-ele, ...), custom_call_target="tpu_custom_call" | custom-call | tf_op jit(solution)/shard_map/unpack/pallas_call | solution.py:877
Async XLA Ops:
  171.4 1.9 %copy-start = (f32[1024,768]{1,0:T(8,128)S(1)}, f32[1024,768]{1,0:T(8,128)}, u32[]{:S(2)}) copy-start(f32[1024,768]{1,0:T(8,128)} %get-tuple-element.41.grad_in) | copy-start | bytes 9437188
  173.3 1.4 copy-start.1
  174.7 0.8 copy-start.2

commit v4 on v3

--- a/solution.py
+++ b/solution.py
@@ -13,7 +13,13 @@
 SHARDS = 16
 ROWS = 48
 LANES = 128
-LAG = 2
+LAG = 4
+HEAD_START = 2
+EACH = 2
+NORM_TICKS = 2
+OUT_TICKS = 2
+PAIR_TICKS = 2
+QKV_TICKS = 2
 DELAY = 0
 MESH = pl.DeviceIdType.MESH
 F32 = jnp.float32
@@ -262,8 +268,9 @@
             store(piece).start()
             for earlier in early_sends:
                 copy(piece, earlier).wait_send()
-
-    early_sends = range(halving)
+            pair_copy(piece).wait_send()
+
+    early_sends = [step for step in range(sends - 1) if not halving <= step < bits]
 
     def offset_of(step):
         return LAG * step + (DELAY if step >= bits else 0)
@@ -492,6 +499,8 @@
             cols = slice(part * 256, (part + 1) * 256)
             hand_in(target, first + size.block, matmul(flip[...], dy_s[:, cols]), "out", part)
         slots(1)
+        if half == 0:
+            slots(2)
         ffn[...] += matmul(act[...], wb[half, units, :])
         dn2[...] += matmul_right(dpre[...], wi[half, :, units])
         sums = matmul(ones, dpre[...])[0:1]
@@ -500,15 +509,13 @@
     def feed_both(chunk, carry):
         def slots(offset, half):
             def place(index):
-                if index == 0:
-                    first = 1 + (chunk - 1) * 4 + offset
-                    lax.fori_loop(first, jnp.where(chunk > 0, first + 1, first), tick, 0)
-                elif half == 1:
+                first = HEAD_START + (chunk - 1) * 4 * EACH + (offset + index) * EACH
+                if index == 1 and half == 1:
                     send_pairs(chunk * size.per_chunk, size.per_chunk)
-                    first = 2 + (chunk - 1) * 4
-                    lax.fori_loop(first, jnp.where(chunk > 0, first + 1, first), tick, 0)
+                if index == 2:
+                    lax.fori_loop(0, jnp.where(chunk > 0, 0, HEAD_START), tick, 0)
                 else:
-                    ticks(chunk * 4, 1)
+                    lax.fori_loop(first, jnp.where(chunk > 0, first + EACH, first), tick, 0)
 
             return place
 
@@ -517,7 +524,7 @@
         return carry
 
     lax.fori_loop(0, size.chunks, feed_both, 0)
-    time = 4 * size.chunks - 3
+    time = HEAD_START + (size.chunks - 1) * 4 * EACH
 
     tiny = 64
 
@@ -568,8 +575,8 @@
     result_copies = row_copies(result, out_rows, 0)
     for item in result_copies:
         item.start()
-    ticks(time, 1)
-    time += 1
+    ticks(time, NORM_TICKS)
+    time += NORM_TICKS
 
     flip[...] = mixed[...].T
     for part in range(width // 256):
@@ -579,8 +586,8 @@
         hand_in(other, size.first_out, grad[local:], "out", part)
     send_pairs(size.first_out, size.first_qkv - size.first_out)
     dmixed[...] = matmul_right(dattn[...], wo[...]).astype(BF16)
-    ticks(time, 1)
-    time += 1
+    ticks(time, OUT_TICKS)
+    time += OUT_TICKS
 
     def attend_back(index, carry):
         half, place = lax.div(index, pairs_half), lax.rem(index, pairs_half)
@@ -611,11 +618,11 @@
         qkv[half, :, columns(place, 0)] = (dquery * scale).astype(BF16)
         qkv[half, :, columns(place, 1)] = dkey.astype(BF16)
         qkv[half, :, columns(place, 2)] = dvalue.astype(BF16)
-        ticks(time + index, 1)
+        ticks(time + index * PAIR_TICKS, PAIR_TICKS)
         return carry
 
     lax.fori_loop(0, 2 * pairs_half, attend_back, 0)
-    time += 2 * pairs_half
+    time += 2 * pairs_half * PAIR_TICKS
 
     flip[...] = normed[...].T
     for half in (1, 0):
@@ -626,16 +633,17 @@
             target[size.first_qkv + part] = grad.astype(BF16).reshape(SHARDS, ROWS, LANES)
         if half == 1:
             send_pairs(size.first_qkv, size.pieces - size.first_qkv)
-        ticks(time, 1)
-        time += 1
+        amount = min(QKV_TICKS, size.first_qkv - time) if half == 1 else QKV_TICKS + 1
+        ticks(time, amount)
+        time += amount
     for half in range(2):
         table = vec if half == 0 else vec_other
         table[6:7, 0:local] = matmul(ones, qkv[half, :, 0:local])[0:1]
         table[6:7, local : 2 * local] = matmul(ones, qkv[half, :, 2 * local : 3 * local])[0:1]
     hidden[...] = matmul_right(qkv[0], wqkv[0])
     hidden[...] += matmul_right(qkv[1], wqkv[1])
-    ticks(time, 1)
-    time += 1
+    ticks(time, QKV_TICKS)
+    time += QKV_TICKS
 
     def first_back(tile, carry):
         sum_gain, sum_shift = carry
@@ -678,9 +686,7 @@
     ticks(time, pieces + offset_of(sends) - time)
 
     def finish(piece, carry):
-        pair_copy(piece).wait_send()
-        for step in range(bits, sends):
-            copy(piece, step).wait_send()
+        copy(piece, sends - 1).wait_send()
         store(piece).wait()
         return carry
 
@@ -894,7 +900,7 @@
             pltpu.SemaphoreType.DMA((transfers,)),
             pltpu.SemaphoreType.DMA((3,)),
         ],
-        compiler_params=pltpu.CompilerParams(vmem_limit_bytes=48 << 20),
+        compiler_params=pltpu.CompilerParams(vmem_limit_bytes=67043328),
         name="unpack",
     )(pieces, vectors, block_rows, grad_rows)
 

time: 185 us -> 169 us (0.914)
  Pallas kernels: 180 us -> 167 us
  local copies, waits for them, and re-layouts: 4.09 us -> 0 us
    pallas_call x1, Pallas kernels: 171 us -> 157 us  [run_layer(): pl.pallas_call(functools.partial(layer_kernel, size), out_shape=(jax.Shap...]
    unnamed x6 -> x0, local copies, waits for them, and re-layouts: 4.09 us -> none
where the time goes in v4:
time: 169 us; the launch traced here: 168 us
  Pallas kernels  167 us (99%)
    pallas_call x1, Pallas kernels, run_layer(): pl.pallas_call(functools.partial(layer_kernel, size), out_shape=(jax.Shap...  157 us
    pallas_call x1, Pallas kernels, unpack(): pl.pallas_call(functools.partial(unpack_kernel, size), out_shape=tuple((j...  10.3 us

profile of v4, /device:TPU:0, one launch (start us, length us, event | category | flops | bytes accessed | tf_op | source)
XLA Modules:
  0.0 168.3 jit_solution(7133249968089584069)
XLA Ops:
  0.7 157.2 %layer.1 = (bf16[1024,768]{1,0:T(8,128)(2,1)}, f32[1024,768]{1,0:T(8,128)}, bf16[36,16,48,128]{3,2,1,0:T(8,128)(2,1)}, f32[16,768]{1,0:T(8,128)}) custom-call(bf16[1024,768]{1,0:T(8,128)(2,1)} %tokens.1, bf16[1024,768]{1,0:T(8,128)(2,1)} %cotangent.1, bf16[768,384]{1,0:T(8,128)(2,1)} %w_query.1, bf16[768,384]{1,0:T(8,128)(2,1)} %w_key.1, ...), custom_call_target="tpu_custom_call" | custom-call | tf_op jit(solution)/shard_map/layer/pallas_call | solution.py:760
  157.9 10.3 %unpack.1 = (f32[768,384]{1,0:T(8,128)}, f32[768,384]{1,0:T(8,128)}, f32[768,384]{1,0:T(8,128)}, f32[384,768]{1,0:T(8,128)}, f32[768,1536]{1,0:T(8,128)}, /*inde...) custom-call(bf16[36,16,48,128]{3,2,1,0:T(8,128)(2,1)} %get-tuple-ele, ...), custom_call_target="tpu_custom_call" | custom-call | tf_op jit(solution)/shard_map/unpack/pallas_call | solution.py:883

commit v5 on v4

--- a/solution.py
+++ b/solution.py
@@ -135,7 +135,6 @@
     wide_b,
     dattn,
     dmixed,
-    result,
     probs_t,
     dscores_t,
     held,
@@ -352,7 +351,7 @@
     ffn[...] = jnp.zeros_like(ffn)
     dn2[...] = jnp.zeros_like(dn2)
 
-    small = 128
+    small = 256
     loads[0].wait()
 
     def first_norm(tile, carry):
@@ -439,7 +438,7 @@
     gathers[8].wait_recv()
     ones = jnp.ones((16, SEQ), BF16)
     fine = 32
-    tall = 256
+    tall = 512
 
     def hand_in(target, first, grad, kind, part):
         wide = 2 * LANES
@@ -526,13 +525,13 @@
     lax.fori_loop(0, size.chunks, feed_both, 0)
     time = HEAD_START + (size.chunks - 1) * 4 * EACH
 
-    tiny = 64
+    tiny = 128
 
     def second_back(tile, carry):
         sum_gain, sum_shift, sum_out = carry
         rows = pl.ds(pl.multiple_of(tile * tiny, tiny), tiny)
         whole = hidden[rows]
-        result[rows] = (whole + (ffn[rows] + row_of(b_back))).astype(BF16)
+        act[rows] = (whole + (ffn[rows] + row_of(b_back))).astype(BF16)
         unit, rstd = norm_parts(whole)
         grad = dn2[rows]
         dhidden = dy_s[rows].astype(F32) + norm_back(grad * row_of(gain_ffn), unit, rstd)
@@ -572,7 +571,7 @@
             ),
         )
 
-    result_copies = row_copies(result, out_rows, 0)
+    result_copies = row_copies(act, out_rows, 0)
     for item in result_copies:
         item.start()
     ticks(time, NORM_TICKS)
@@ -729,9 +728,8 @@
         pltpu.VMEM((SEQ, width), BF16),
         pltpu.VMEM((SEQ, width), BF16),
         pltpu.VMEM((width, SEQ), BF16),
-        pltpu.VMEM((256, width), F32),
-        pltpu.VMEM((256, width), F32),
-        pltpu.VMEM((SEQ, width), BF16),
+        pltpu.VMEM((SEQ, width), F32),
+        pltpu.VMEM((SEQ, width), F32),
         pltpu.VMEM((SEQ, width), BF16),
         pltpu.VMEM((SEQ, width), BF16),
         pltpu.VMEM((LANES // HEAD, SEQ, SEQ), BF16),

time: 169 us -> 167 us (0.988)
  Pallas kernels: 167 us -> 165 us
    pallas_call x1, Pallas kernels: 157 us -> 155 us  [run_layer(): pl.pallas_call(functools.partial(layer_kernel, size), out_shape=(jax.Shap...]
where the time goes in v5:
time: 167 us; the launch traced here: 166 us
  Pallas kernels  165 us (99%)
    pallas_call x1, Pallas kernels, run_layer(): pl.pallas_call(functools.partial(layer_kernel, size), out_shape=(jax.Shap...  155 us
    pallas_call x1, Pallas kernels, unpack(): pl.pallas_call(functools.partial(unpack_kernel, size), out_shape=tuple((j...  10.3 us

profile of v5, /device:TPU:0, one launch (start us, length us, event | category | flops | bytes accessed | tf_op | source)
XLA Modules:
  0.0 166.3 jit_solution(14581957282532510839)
XLA Ops:
  0.7 155.2 %layer.1 = (bf16[1024,768]{1,0:T(8,128)(2,1)}, f32[1024,768]{1,0:T(8,128)}, bf16[36,16,48,128]{3,2,1,0:T(8,128)(2,1)}, f32[16,768]{1,0:T(8,128)}) custom-call(bf16[1024,768]{1,0:T(8,128)(2,1)} %tokens.1, bf16[1024,768]{1,0:T(8,128)(2,1)} %cotangent.1, bf16[768,384]{1,0:T(8,128)(2,1)} %w_query.1, bf16[768,384]{1,0:T(8,128)(2,1)} %w_key.1, ...), custom_call_target="tpu_custom_call" | custom-call | tf_op jit(solution)/shard_map/layer/pallas_call | solution.py:758
  155.9 10.3 %unpack.1 = (f32[768,384]{1,0:T(8,128)}, f32[768,384]{1,0:T(8,128)}, f32[768,384]{1,0:T(8,128)}, f32[384,768]{1,0:T(8,128)}, f32[768,1536]{1,0:T(8,128)}, /*inde...) custom-call(bf16[36,16,48,128]{3,2,1,0:T(8,128)(2,1)} %get-tuple-ele, ...), custom_call_target="tpu_custom_call" | custom-call | tf_op jit(solution)/shard_map/unpack/pallas_call | solution.py:881
